TPU v7x, 32 devices: a whole 2x2x4 slice. The times are simulated.
32 devices in a mesh: cand: 4 (over x, core), seq: 8 (over z, y).
Axes of the slice: x: 2, y: 2, z: 4, core: 2. Of those that a mesh axis runs over, the one named last changes fastest.
Arguments:
- response_query_array: bfloat16 [8, 768, 2560], P('cand', 'seq'), may hold values from -180 to 180
- response_key_array: bfloat16 [8, 768, 512], P('cand', 'seq'), may hold values from -6 to 6
- response_value_array: bfloat16 [8, 768, 512], P('cand', 'seq'), may hold values from -6 to 6
- prompt_key_array: bfloat16 [2048, 512], P(('cand', 'seq')), may hold values from -6 to 6
- prompt_value_array: bfloat16 [2048, 512], P(('cand', 'seq')), may hold values from -6 to 6
- lengths: int32 [8], replicated, may hold values from 192 to 768, as said below
- offsets: int32 [8], replicated, may hold values from 512 to 2048, as said below
- ranks: int32 [8], replicated, may hold values from 0 to 7, each once
Outputs:
- attention: bfloat16 [8, 768, 2560], P('cand', 'seq')
Inputs may be any that keep to these rules, and one draw needn't show every extreme that they name: `lengths`: some candidate's response has all 768 positions live. `offsets`: some candidate sees the whole prompt.
All inputs are finite; a program needn't handle non-finite values.
Results may differ from a plain program's by a relative error of at most 0.004.
Values may be sent and summed in bfloat16 or wider, within the bound.
No kernel may reach another device: no remote copies, remote signals or barrier semaphores. Data moves between devices by JAX's collectives and lax.ppermute only.
A program may use at most 128 MiB of HBM per device.

v0:
```python
import math

import jax
import jax.numpy as jnp
from jax import lax
from jax.sharding import PartitionSpec as P

QUERY_HEADS = 20
KEY_VALUE_HEADS = 4
HEAD_DIMENSION = 128


lowest_score_value = -1e30


def attend_block(running, query_rows, block_keys, block_values, allowed, shared):
    running_max, running_total, running_sum = running
    cand_count = query_rows.shape[0]
    heads_kv = query_rows.shape[2]
    head_size = query_rows.shape[4]
    score_scale = 1.0 / math.sqrt(head_size)
    if shared:
        keys_split = block_keys.reshape(block_keys.shape[0], heads_kv, head_size)
        values_split = block_values.reshape(block_values.shape[0], heads_kv, head_size)
        scores = jnp.einsum(
            "crhgd,nhd->chgrn", query_rows, keys_split, preferred_element_type=jnp.float32
        )
    else:
        keys_split = block_keys.reshape(cand_count, block_keys.shape[1], heads_kv, head_size)
        values_split = block_values.reshape(cand_count, block_values.shape[1], heads_kv, head_size)
        scores = jnp.einsum(
            "crhgd,cnhd->chgrn", query_rows, keys_split, preferred_element_type=jnp.float32
        )
    scores = jnp.where(allowed[:, None, None, :, :], scores * score_scale, -jnp.inf)
    new_max = jnp.maximum(running_max, jnp.max(scores, axis=-1))
    rescale = jnp.exp(running_max - new_max)
    exponent = jnp.exp(scores - new_max[..., None])
    weights = exponent.astype(jnp.bfloat16)
    new_total = running_total * rescale + jnp.sum(exponent, axis=-1)
    if shared:
        contrib = jnp.einsum(
            "chgrn,nhd->chgrd", weights, values_split, preferred_element_type=jnp.float32
        )
    else:
        contrib = jnp.einsum(
            "chgrn,cnhd->chgrd", weights, values_split, preferred_element_type=jnp.float32
        )
    new_sum = running_sum * rescale[..., None] + contrib
    return (new_max, new_total, new_sum)


def fold_blocks(
    running, query_rows, all_keys, all_values, key_pos, allowed_of, shared, live_of=None
):
    key_count = key_pos.shape[0]
    block_len = math.gcd(key_count, 512)
    keys_axis = 0 if shared else 1

    def one_block(step_at, carried):
        block_start = step_at * block_len
        block_keys = lax.dynamic_slice_in_dim(all_keys, block_start, block_len, keys_axis)
        block_values = lax.dynamic_slice_in_dim(all_values, block_start, block_len, keys_axis)
        block_pos = lax.dynamic_slice_in_dim(key_pos, block_start, block_len, 0)
        return attend_block(
            carried, query_rows, block_keys, block_values, allowed_of(block_pos), shared
        )

    return lax.fori_loop(0, key_count // block_len, one_block, running)


def body(
    response_query_array,
    response_key_array,
    response_value_array,
    prompt_key_array,
    prompt_value_array,
    lengths,
    offsets,
    ranks,
):
    candidate_local, output_rows, width = response_query_array.shape
    group_width = QUERY_HEADS // KEY_VALUE_HEADS
    group_at = lax.axis_index("cand")
    seq_at = lax.axis_index("seq")
    first_cand = group_at * candidate_local
    my_lengths = lax.dynamic_slice_in_dim(lengths, first_cand, candidate_local)
    my_offsets = lax.dynamic_slice_in_dim(offsets, first_cand, candidate_local)
    query_pos = seq_at * output_rows + jnp.arange(output_rows, dtype=jnp.int32)
    query_rows = response_query_array.reshape(
        candidate_local, output_rows, KEY_VALUE_HEADS, group_width, HEAD_DIMENSION
    )
    pieces = (
        lax.all_gather(prompt_key_array, ("cand", "seq"), axis=0, tiled=True),
        lax.all_gather(prompt_value_array, ("cand", "seq"), axis=0, tiled=True),
    )
    key_pos = jnp.arange(pieces[0].shape[0], dtype=jnp.int32)

    def allowed_of(block_pos):
        return block_pos[None, None, :] < my_offsets[:, None, None]

    running = fold_blocks(
        (
            jnp.full(
                (candidate_local, KEY_VALUE_HEADS, group_width, output_rows),
                lowest_score_value,
                jnp.float32,
            ),
            jnp.zeros((candidate_local, KEY_VALUE_HEADS, group_width, output_rows), jnp.float32),
            jnp.zeros(
                (candidate_local, KEY_VALUE_HEADS, group_width, output_rows, HEAD_DIMENSION),
                jnp.float32,
            ),
        ),
        query_rows,
        pieces[0],
        pieces[1],
        key_pos,
        allowed_of,
        True,
    )
    pieces = (
        lax.all_gather(response_key_array, "seq", axis=1, tiled=True),
        lax.all_gather(response_value_array, "seq", axis=1, tiled=True),
    )
    key_pos = jnp.arange(pieces[0].shape[1], dtype=jnp.int32)

    def allowed_of(block_pos):
        causal = block_pos[None, None, :] <= query_pos[None, :, None]
        return causal & (block_pos[None, None, :] < my_lengths[:, None, None])

    final_max, final_total, final_sum = fold_blocks(
        running, query_rows, pieces[0], pieces[1], key_pos, allowed_of, False
    )
    attended = final_sum / final_total[..., None]
    attended = jnp.transpose(attended, (0, 3, 1, 2, 4)).reshape(candidate_local, output_rows, width)
    row_valid = query_pos[None, :] < my_lengths[:, None]
    attended = jnp.where(row_valid[:, :, None], attended, 0.0).astype(jnp.bfloat16)
    gathered = lax.all_gather(attended, "cand", axis=0, tiled=True)
    every_cand = jnp.arange(gathered.shape[0], dtype=jnp.int32)
    chosen = []
    for within in range(candidate_local):
        target = first_cand + within
        source = jnp.sum(jnp.where(ranks == target, every_cand, 0))
        chosen.append(lax.dynamic_index_in_dim(gathered, source, 0, keepdims=False))
    return jnp.stack(chosen, axis=0)


def solution(mesh):
    in_specs = (
        P("cand", "seq", None),
        P("cand", "seq", None),
        P("cand", "seq", None),
        P(("cand", "seq"), None),
        P(("cand", "seq"), None),
        P(),
        P(),
        P(),
    )
    out_specs = P("cand", "seq", None)
    return jax.shard_map(body, mesh=mesh, in_specs=in_specs, out_specs=out_specs, check_vma=False)
```

profile of v0, /device:TPU:0, one launch (start us, length us, event | category | flops | bytes accessed | tf_op | source)
XLA Modules:
  0.0 304.9 jit_solution(10088347945177968936)
XLA Ops:
  15.9 53.7 %all-gather.6.cloned.1.call-done = bf16[2048,512]{1,0:T(8,128)(2,1)} async-done(((bf16[64,512]{1,0:T(8,128)(2,1)}), bf16[2048,512]{1,0:T(8,128)(2,1)}) %all-gather.6.cloned.1.call-update) | async-done | bytes 2097168 | tf_op jit(solution)/shard_map/all_gather | solution.py:93
  69.6 58.4 %all-gather.8.cloned.1.call-done = bf16[2048,512]{1,0:T(8,128)(2,1)} async-done(((bf16[64,512]{1,0:T(8,128)(2,1)}), bf16[2048,512]{1,0:T(8,128)(2,1)}) %all-gather.8.cloned.1.call-update) | async-done | bytes 2097168 | tf_op jit(solution)/shard_map/all_gather | solution.py:94
  128.0 65.4 %while.37 = (s32[]{:T(128)}, f32[2,4,5,96]{3,2,0,1:T(8,128)S(1)}, f32[2,4,5,96]{3,2,0,1:T(8,128)S(1)}, f32[2,4,5,96,128]{4,3,2,0,1:T(8,128)}, s32[2048]{0:T(1024...) while((s32[]{:T(128)}, f32[2,4,5,96]{3,2,0,1:T(8,128)S(1)}, ...), condition=%wide.region_3.4_spmd.clone, body=%wide.region_0.3_spmd.clone.sunk | while | flops 1029754624 | bytes 34007236 | solution.py:68
  129.6 4.2 %fusion.60 = (f32[2,4,5,96]{3,2,0,1:T(8,128)S(1)}, f32[4,512,2,96,5]{1,3,4,2,0:T(8,128)}) fusion(pred[2,512]{1,0:T(4,128)(4,1)S(1)} %broadcast_compare_fusion.9, bf16[512,4,128,1,1]{0,2,4,3,1:T(8,128)(2,1)S(1)} %bitcast.88, bf16[2,96,4,5,128]{4,1,3,0,2:T(8,128)(2,1)S(1)} %get-tuple-element.683), kind=kOutput, calls=%fused_computation.26.clone.1 | convolution fusion | flops 509210880 | bytes 9388032 | tf_op jit(solution)/shard_map/while/body/eval_jaxpr/crhgd,nhd->chgrn/dot_general | solution.py:25
  133.9 4.5 %fusion.61 = f32[2,4,5,96]{3,2,0,1:T(8,128)S(1)} fusion(f32[4,512,2,96,5]{1,3,4,2,0:T(8,128)} %get-tuple-element.646, f32[2,4,5,96]{3,2,0,1:T(8,128)S(1)} %select_maximum_fusion.2, pred[2,512]{1,0:T(4,128)(4,1)S(1)} %broadcast_compare_fusion.9), kind=kLoop, calls=%fused_computation.25.clone.1 | loop fusion | flops 7860480 | bytes 7896064 | tf_op jit(solution)/shard_map/while/body/eval_jaxpr/reduce_sum | solution.py:39
  138.6 5.4 %bitcast_add_fusion.2 = f32[2,4,5,96,128]{4,3,2,0,1:T(8,128)} fusion(f32[2,4,5,96,128]{4,3,2,0,1:T(8,128)} %get-tuple-element.666, bf16[512,4,128,1,1]{0,2,4,3,1:T(8,128)(2,1)S(1)} %bitcast.91, f32[4,512,2,96,5]{1,3,4,2,0:T(8,128)} %get-tuple-element.646, f32[2,4,5,96]{3,2,0,1:T(8,128)S(1)} %select_maximum_fusion.2, ...), kind=kOutput, calls=%fused_computation.32.clone.1 | convolution fusion | flops 512655360 | bytes 12352513 | tf_op jit(solution)/shard_map/while/body/eval_jaxpr/chgrn,nhd->chgrd/dot_general | solution.py:41
  145.7 4.2 %fusion.60 = (f32[2,4,5,96]{3,2,0,1:T(8,128)S(1)}, f32[4,512,2,96,5]{1,3,4,2,0:T(8,128)}) fusion(pred[2,512]{1,0:T(4,128)(4,1)S(1)} %broadcast_compare_fusion.9, bf16[512,4,128,1,1]{0,2,4,3,1:T(8,128)(2,1)S(1)} %bitcast.88, bf16[2,96,4,5,128]{4,1,3,0,2:T(8,128)(2,1)S(1)} %get-tuple-element.683), kind=kOutput, calls=%fused_computation.26.clone.1 | convolution fusion | flops 509210880 | bytes 9388032 | tf_op jit(solution)/shard_map/while/body/eval_jaxpr/crhgd,nhd->chgrn/dot_general | solution.py:25
  149.9 4.4 %fusion.61 = f32[2,4,5,96]{3,2,0,1:T(8,128)S(1)} fusion(f32[4,512,2,96,5]{1,3,4,2,0:T(8,128)} %get-tuple-element.646, f32[2,4,5,96]{3,2,0,1:T(8,128)S(1)} %select_maximum_fusion.2, pred[2,512]{1,0:T(4,128)(4,1)S(1)} %broadcast_compare_fusion.9), kind=kLoop, calls=%fused_computation.25.clone.1 | loop fusion | flops 7860480 | bytes 7896064 | tf_op jit(solution)/shard_map/while/body/eval_jaxpr/reduce_sum | solution.py:39
  154.6 6.0 %bitcast_add_fusion.2 = f32[2,4,5,96,128]{4,3,2,0,1:T(8,128)} fusion(f32[2,4,5,96,128]{4,3,2,0,1:T(8,128)} %get-tuple-element.666, bf16[512,4,128,1,1]{0,2,4,3,1:T(8,128)(2,1)S(1)} %bitcast.91, f32[4,512,2,96,5]{1,3,4,2,0:T(8,128)} %get-tuple-element.646, f32[2,4,5,96]{3,2,0,1:T(8,128)S(1)} %select_maximum_fusion.2, ...), kind=kOutput, calls=%fused_computation.32.clone.1 | convolution fusion | flops 512655360 | bytes 12352513 | tf_op jit(solution)/shard_map/while/body/eval_jaxpr/chgrn,nhd->chgrd/dot_general | solution.py:41
  162.2 4.2 %fusion.60 = (f32[2,4,5,96]{3,2,0,1:T(8,128)S(1)}, f32[4,512,2,96,5]{1,3,4,2,0:T(8,128)}) fusion(pred[2,512]{1,0:T(4,128)(4,1)S(1)} %broadcast_compare_fusion.9, bf16[512,4,128,1,1]{0,2,4,3,1:T(8,128)(2,1)S(1)} %bitcast.88, bf16[2,96,4,5,128]{4,1,3,0,2:T(8,128)(2,1)S(1)} %get-tuple-element.683), kind=kOutput, calls=%fused_computation.26.clone.1 | convolution fusion | flops 509210880 | bytes 9388032 | tf_op jit(solution)/shard_map/while/body/eval_jaxpr/crhgd,nhd->chgrn/dot_general | solution.py:25
  166.4 4.4 %fusion.61 = f32[2,4,5,96]{3,2,0,1:T(8,128)S(1)} fusion(f32[4,512,2,96,5]{1,3,4,2,0:T(8,128)} %get-tuple-element.646, f32[2,4,5,96]{3,2,0,1:T(8,128)S(1)} %select_maximum_fusion.2, pred[2,512]{1,0:T(4,128)(4,1)S(1)} %broadcast_compare_fusion.9), kind=kLoop, calls=%fused_computation.25.clone.1 | loop fusion | flops 7860480 | bytes 7896064 | tf_op jit(solution)/shard_map/while/body/eval_jaxpr/reduce_sum | solution.py:39
  171.1 5.9 %bitcast_add_fusion.2 = f32[2,4,5,96,128]{4,3,2,0,1:T(8,128)} fusion(f32[2,4,5,96,128]{4,3,2,0,1:T(8,128)} %get-tuple-element.666, bf16[512,4,128,1,1]{0,2,4,3,1:T(8,128)(2,1)S(1)} %bitcast.91, f32[4,512,2,96,5]{1,3,4,2,0:T(8,128)} %get-tuple-element.646, f32[2,4,5,96]{3,2,0,1:T(8,128)S(1)} %select_maximum_fusion.2, ...), kind=kOutput, calls=%fused_computation.32.clone.1 | convolution fusion | flops 512655360 | bytes 12352513 | tf_op jit(solution)/shard_map/while/body/eval_jaxpr/chgrn,nhd->chgrd/dot_general | solution.py:41
  178.6 4.2 %fusion.60 = (f32[2,4,5,96]{3,2,0,1:T(8,128)S(1)}, f32[4,512,2,96,5]{1,3,4,2,0:T(8,128)}) fusion(pred[2,512]{1,0:T(4,128)(4,1)S(1)} %broadcast_compare_fusion.9, bf16[512,4,128,1,1]{0,2,4,3,1:T(8,128)(2,1)S(1)} %bitcast.88, bf16[2,96,4,5,128]{4,1,3,0,2:T(8,128)(2,1)S(1)} %get-tuple-element.683), kind=kOutput, calls=%fused_computation.26.clone.1 | convolution fusion | flops 509210880 | bytes 9388032 | tf_op jit(solution)/shard_map/while/body/eval_jaxpr/crhgd,nhd->chgrn/dot_general | solution.py:25
  182.8 4.4 %fusion.61 = f32[2,4,5,96]{3,2,0,1:T(8,128)S(1)} fusion(f32[4,512,2,96,5]{1,3,4,2,0:T(8,128)} %get-tuple-element.646, f32[2,4,5,96]{3,2,0,1:T(8,128)S(1)} %select_maximum_fusion.2, pred[2,512]{1,0:T(4,128)(4,1)S(1)} %broadcast_compare_fusion.9), kind=kLoop, calls=%fused_computation.25.clone.1 | loop fusion | flops 7860480 | bytes 7896064 | tf_op jit(solution)/shard_map/while/body/eval_jaxpr/reduce_sum | solution.py:39
  187.5 5.9 %bitcast_add_fusion.2 = f32[2,4,5,96,128]{4,3,2,0,1:T(8,128)} fusion(f32[2,4,5,96,128]{4,3,2,0,1:T(8,128)} %get-tuple-element.666, bf16[512,4,128,1,1]{0,2,4,3,1:T(8,128)(2,1)S(1)} %bitcast.91, f32[4,512,2,96,5]{1,3,4,2,0:T(8,128)} %get-tuple-element.646, f32[2,4,5,96]{3,2,0,1:T(8,128)S(1)} %select_maximum_fusion.2, ...), kind=kOutput, calls=%fused_computation.32.clone.1 | convolution fusion | flops 512655360 | bytes 12352513 | tf_op jit(solution)/shard_map/while/body/eval_jaxpr/chgrn,nhd->chgrd/dot_general | solution.py:41
  196.3 22.1 %all-gather.12.cloned.1.call-done = bf16[2,768,512]{2,0,1:T(2,128)(2,1)} async-done(((bf16[2,96,512]{2,0,1:T(2,128)(2,1)}), bf16[2,768,512]{2,0,1:T(2,128)(2,1)}) %all-gather.12.cloned.1.call-update) | async-done | bytes 1572880 | tf_op jit(solution)/shard_map/all_gather | solution.py:123
  218.4 41.8 %while.36 = (s32[]{:T(128)}, f32[2,4,5,96]{3,2,1,0:T(8,128)}, f32[2,4,5,96]{3,2,1,0:T(8,128)}, f32[2,4,5,96,128]{4,3,2,1,0:T(8,128)S(1)}, s32[768]{0:T(1024)S(1)...) while((s32[]{:T(128)}, f32[2,4,5,96]{3,2,1,0:T(8,128)}, ...), condition=%wide.region_7.8_spmd.clone, body=%wide.region_4.7_spmd.clone.sunk | while | flops 515194976 | bytes 38561872 | solution.py:68
  221.8 2.2 fusion.54
  228.0 3.7 %multiply_add_fusion.5 = f32[2,4,5,96,128]{4,3,2,1,0:T(8,128)S(1)} fusion(f32[2,4,5,96,128]{4,3,2,1,0:T(8,128)S(1)} %get-tuple-element.706, bf16[2,256,4,128,1]{1,3,4,2,0:T(8,128)(2,1)S(1)} %bitcast.89, f32[2,4,256,96,5]{2,3,4,1,0:T(8,128)} %copy-done, f32[2,4,5,96]{3,2,1,0:T(8,128)S(1)} %max.19, pred[2,96,256]{2,1,0:T(8,128)(4,1)S(1)} %copy-done.1, ...), kind=kOutput, calls=%fused_computation.7.clone.1 | convolution fusion | flops 256573440 | bytes 8468480 | tf_op jit(solution)/shard_map/while/body/eval_jaxpr/chgrn,cnhd->chgrd/dot_general | solution.py:45
  235.7 2.2 fusion.54
  241.9 3.7 %multiply_add_fusion.5 = f32[2,4,5,96,128]{4,3,2,1,0:T(8,128)S(1)} fusion(f32[2,4,5,96,128]{4,3,2,1,0:T(8,128)S(1)} %get-tuple-element.706, bf16[2,256,4,128,1]{1,3,4,2,0:T(8,128)(2,1)S(1)} %bitcast.89, f32[2,4,256,96,5]{2,3,4,1,0:T(8,128)} %copy-done, f32[2,4,5,96]{3,2,1,0:T(8,128)S(1)} %max.19, pred[2,96,256]{2,1,0:T(8,128)(4,1)S(1)} %copy-done.1, ...), kind=kOutput, calls=%fused_computation.7.clone.1 | convolution fusion | flops 256573440 | bytes 8468480 | tf_op jit(solution)/shard_map/while/body/eval_jaxpr/chgrn,cnhd->chgrd/dot_general | solution.py:45
  249.7 2.2 fusion.54
  255.9 3.7 %multiply_add_fusion.5 = f32[2,4,5,96,128]{4,3,2,1,0:T(8,128)S(1)} fusion(f32[2,4,5,96,128]{4,3,2,1,0:T(8,128)S(1)} %get-tuple-element.706, bf16[2,256,4,128,1]{1,3,4,2,0:T(8,128)(2,1)S(1)} %bitcast.89, f32[2,4,256,96,5]{2,3,4,1,0:T(8,128)} %copy-done, f32[2,4,5,96]{3,2,1,0:T(8,128)S(1)} %max.19, pred[2,96,256]{2,1,0:T(8,128)(4,1)S(1)} %copy-done.1, ...), kind=kOutput, calls=%fused_computation.7.clone.1 | convolution fusion | flops 256573440 | bytes 8468480 | tf_op jit(solution)/shard_map/while/body/eval_jaxpr/chgrn,cnhd->chgrd/dot_general | solution.py:45
  268.5 27.6 %all-gather.14.cloned.1.call-done = bf16[8,96,2560]{2,1,0:T(8,128)(2,1)} async-done(((bf16[2,96,2560]{2,1,0:T(8,128)(2,1)}), bf16[8,96,2560]{2,1,0:T(8,128)(2,1)}) %all-gather.14.cloned.1.call-update) | async-done | bytes 3932176 | tf_op jit(solution)/shard_map/all_gather | solution.py:138
  (139 shorter events, 50.3 us)
Async XLA Ops:
  6.5 63.1 %all-gather.6.cloned.1.call-start = ((), (), s32[]{:S(2)}) async-start(), calls=%async_computation | async-start | bytes 2162688 | tf_op jit(solution)/shard_map/all_gather | solution.py:93
  7.3 120.7 %all-gather.8.cloned.1.call-start = ((), (), s32[]{:S(2)}) async-start(), calls=%async_computation.1 | async-start | bytes 2162688 | tf_op jit(solution)/shard_map/all_gather | solution.py:94
  8.0 188.3 %all-gather.10.cloned.1.call-start = ((), (), s32[]{:S(2)}) async-start(), calls=%async_computation.2 | async-start | bytes 1769472 | tf_op jit(solution)/shard_map/all_gather | solution.py:122
  9.9 5.8 %copy-start.6 = (s32[8]{0:T(128)S(1)}, s32[8]{0:T(128)}, u32[]{:S(2)}) copy-start(s32[8]{0:T(128)} %param.18) | copy-start | bytes 100
  9.9 5.9 %copy-start.7 = (s32[8]{0:T(128)S(1)}, s32[8]{0:T(128)}, u32[]{:S(2)}) copy-start(s32[8]{0:T(128)} %param.17) | copy-start | bytes 100
  9.9 208.5 %all-gather.12.cloned.1.call-start = ((), (), s32[]{:S(2)}) async-start(), calls=%async_computation.3 | async-start | bytes 1769472 | tf_op jit(solution)/shard_map/all_gather | solution.py:123
  11.8 284.3 %all-gather.14.cloned.1.call-start = ((), (), s32[]{:S(2)}) async-start(), calls=%async_computation.4 | async-start | bytes 4915200 | tf_op jit(solution)/shard_map/all_gather | solution.py:138
  221.8 2.2 copy-start.2
  221.8 4.1 %copy-start.1 = (pred[2,96,256]{2,1,0:T(8,128)(4,1)S(1)}, pred[2,96,256]{2,1,0:T(8,128)(4,1)}, u32[]{:S(2)}) copy-start(pred[2,96,256]{2,1,0:T(8,128)(4,1)} %broadcast_and_fusion.2) | copy-start | bytes 147460 | tf_op jit(solution)/shard_map/while
  221.8 5.6 %copy-start.3 = (f32[2,4,5,96]{3,2,1,0:T(8,128)S(1)}, f32[2,4,5,96]{3,2,1,0:T(8,128)}, u32[]{:S(2)}) copy-start(f32[2,4,5,96]{3,2,1,0:T(8,128)} %get-tuple-element.705) | copy-start | bytes 46084 | tf_op jit(solution)/shard_map/while
  224.0 1.8 copy-start
  227.4 4.3 %copy-start.4 = (f32[2,4,5,96]{3,2,1,0:T(8,128)}, f32[2,4,5,96]{3,2,1,0:T(8,128)S(1)}, u32[]{:S(2)}) copy-start(f32[2,4,5,96]{3,2,1,0:T(8,128)S(1)} %get-tuple-element.719) | copy-start | bytes 46084 | tf_op jit(solution)/shard_map/while
  235.7 2.2 copy-start.2
  235.7 4.1 %copy-start.1 = (pred[2,96,256]{2,1,0:T(8,128)(4,1)S(1)}, pred[2,96,256]{2,1,0:T(8,128)(4,1)}, u32[]{:S(2)}) copy-start(pred[2,96,256]{2,1,0:T(8,128)(4,1)} %broadcast_and_fusion.2) | copy-start | bytes 147460 | tf_op jit(solution)/shard_map/while
  235.7 5.6 %copy-start.3 = (f32[2,4,5,96]{3,2,1,0:T(8,128)S(1)}, f32[2,4,5,96]{3,2,1,0:T(8,128)}, u32[]{:S(2)}) copy-start(f32[2,4,5,96]{3,2,1,0:T(8,128)} %get-tuple-element.705) | copy-start | bytes 46084 | tf_op jit(solution)/shard_map/while
  237.9 1.8 copy-start
  241.4 4.3 %copy-start.4 = (f32[2,4,5,96]{3,2,1,0:T(8,128)}, f32[2,4,5,96]{3,2,1,0:T(8,128)S(1)}, u32[]{:S(2)}) copy-start(f32[2,4,5,96]{3,2,1,0:T(8,128)S(1)} %get-tuple-element.719) | copy-start | bytes 46084 | tf_op jit(solution)/shard_map/while
  249.6 2.2 copy-start.2
  249.6 4.1 %copy-start.1 = (pred[2,96,256]{2,1,0:T(8,128)(4,1)S(1)}, pred[2,96,256]{2,1,0:T(8,128)(4,1)}, u32[]{:S(2)}) copy-start(pred[2,96,256]{2,1,0:T(8,128)(4,1)} %broadcast_and_fusion.2) | copy-start | bytes 147460 | tf_op jit(solution)/shard_map/while
  249.7 5.6 %copy-start.3 = (f32[2,4,5,96]{3,2,1,0:T(8,128)S(1)}, f32[2,4,5,96]{3,2,1,0:T(8,128)}, u32[]{:S(2)}) copy-start(f32[2,4,5,96]{3,2,1,0:T(8,128)} %get-tuple-element.705) | copy-start | bytes 46084 | tf_op jit(solution)/shard_map/while
  251.9 1.8 copy-start
  255.3 4.3 %copy-start.4 = (f32[2,4,5,96]{3,2,1,0:T(8,128)}, f32[2,4,5,96]{3,2,1,0:T(8,128)S(1)}, u32[]{:S(2)}) copy-start(f32[2,4,5,96]{3,2,1,0:T(8,128)S(1)} %get-tuple-element.719) | copy-start | bytes 46084 | tf_op jit(solution)/shard_map/while
  261.5 2.6 copy-start.5
Sparse Core Ops, SparseCore 0:
  10.3 59.2 all-gather.5
  72.6 55.3 all-gather.7
  130.2 43.0 all-gather.9
  175.3 43.0 all-gather.11
  264.3 31.7 all-gather.13
where the time goes:
time: 306 us; the launch traced here: 305 us
  waiting for transfers between devices  163 us (53%)
  matrix products  57.7 us (19%)
  local copies, waits for them, and re-layouts  36.7 us (12%)
  other arithmetic  29.6 us (10%)
  between operations  16.9 us (6%)
    all_gather x1, waiting for transfers between devices, body(): lax.all_gather(prompt_value_array, ('cand', 'seq'), axis=0, tiled=True)  58.4 us
    all_gather x1, waiting for transfers between devices, body(): lax.all_gather(prompt_key_array, ('cand', 'seq'), axis=0, tiled=True)  53.7 us
    all_gather x1, waiting for transfers between devices, body(): gathered = lax.all_gather(attended, 'cand', axis=0, tiled=True)  27.6 us
    dot_general x4, matrix products, attend_block(): jnp.einsum('chgrn,nhd->chgrd', weights, values_split, preferred_element_t...  23.1 us
    reduce_sum x7, other arithmetic, attend_block(): new_total = running_total * rescale + jnp.sum(exponent, axis=-1)  22.3 us
    all_gather x1, waiting for transfers between devices, body(): lax.all_gather(response_value_array, 'seq', axis=1, tiled=True)  22.1 us
    dot_general x4, matrix products, attend_block(): jnp.einsum('crhgd,nhd->chgrn', query_rows, keys_split, preferred_element_...  16.9 us
    dynamic_slice x14, local copies, waits for them, and re-layouts, one_block(): lax.dynamic_slice_in_dim(all_values, block_start, block_len, keys_axis)  13.3 us
  transfers between devices with their start and end apart: 5, of which 4 were waited for; matrix products, arithmetic and copies ran while one was open for 25% of the time, Pallas kernels for 0%

commit v1 on v0

v1 whole, which is shorter than its diff:
```python
import functools
import math

import jax
import jax.numpy as jnp
from jax import lax
from jax.experimental import pallas as pl
from jax.experimental.pallas import tpu as pltpu
from jax.sharding import PartitionSpec as P

QUERY_HEADS = 20
KEY_VALUE_HEADS = 4
HEAD = 128
GROUP = QUERY_HEADS // KEY_VALUE_HEADS
WIDE = GROUP * HEAD
SCORE_FACTOR = math.log2(math.e) / math.sqrt(HEAD)
LOWEST = -1e30
AXES = ("cand", "seq")
VMEM_LIMIT = 56 * 1024 * 1024
VMEM = pl.BlockSpec(memory_space=pltpu.VMEM)
SMEM = pl.BlockSpec(memory_space=pltpu.SMEM)

FIELDS = 5


class Layout:
    def __init__(self, mesh):
        assert mesh.shape["cand"] == 4 and mesh.shape["seq"] % 2 == 0
        self.rings = mesh.shape["seq"] // 2

    def permute(self, array, d=0, core=0, ring=0):
        pairs = []
        for x in range(2):
            for c in range(2):
                for r in range(self.rings):
                    for y in range(2):
                        source = ((x * 2 + c) * self.rings + r) * 2 + y
                        target = ((x ^ (d >> 1)) * 2 + (c ^ core)) * self.rings
                        target = (target + (r + ring) % self.rings) * 2 + (y ^ (d & 1))
                        pairs.append((source, target))
        return lax.ppermute(array, AXES, pairs)

    def exchange(self, pieces):
        return [pieces[0]] + [self.permute(pieces[d], d=d) for d in range(1, 4)]

    def ring_gather(self, block):
        pieces = [block]
        for _ in range(self.rings - 1):
            pieces.append(self.permute(pieces[-1], ring=1))
        return pieces


def kernel_call(kernel, out_shape, operands, scratch=(), cost=(0, 0), name=None):
    many = isinstance(out_shape, list)
    return pl.pallas_call(
        kernel,
        out_shape=out_shape,
        in_specs=[SMEM] + [VMEM] * (len(operands) - 1),
        out_specs=[VMEM] * len(out_shape) if many else VMEM,
        scratch_shapes=list(scratch),
        compiler_params=pltpu.CompilerParams(vmem_limit_bytes=VMEM_LIMIT),
        cost_estimate=pl.CostEstimate(
            flops=cost[0], transcendentals=cost[0] // 512, bytes_accessed=cost[1]
        ),
        name=name,
    )(*operands)


def pack_keys_kernel(info, rk, rv, pk, pv, *outs):
    cands, rows = rk.shape[0], rk.shape[1]
    own = info[0] * 2 + info[3]
    for d, out in enumerate(outs):
        lane = pl.ds(pl.multiple_of((own ^ d) * HEAD, HEAD), HEAD)
        for w in range(cands):
            out[w * rows : (w + 1) * rows, :HEAD] = rk[w, :, lane]
            out[w * rows : (w + 1) * rows, HEAD:] = rv[w, :, lane]
        out[cands * rows :, :HEAD] = pk[:, lane]
        out[cands * rows :, HEAD:] = pv[:, lane]


def pack_queries_kernel(info, q, *outs):
    own = info[0] * 2 + info[3]
    for d, out in enumerate(outs):
        lane = pl.ds(pl.multiple_of((own ^ d) * WIDE, HEAD), WIDE)
        for w in range(q.shape[0]):
            out[w] = q[w, :, lane]


def unit_info(info, unit, field):
    return info[4 + unit * FIELDS + field]


def select_keys_kernel(cands, rows, info, own, other, *outs):
    for w, out in enumerate(outs):
        for dx in range(2):
            unit = w * 2 + dx
            away = unit_info(info, unit, 0)
            home = unit_info(info, unit, 1)
            row = pl.ds(pl.multiple_of(unit_info(info, unit, 2) * rows, rows), rows)
            for dy in range(2):
                d = home * 2 + dy
                out[dx, dy] = jnp.where(away == 1, other[d, row, :], own[d, row, :])


def load_queries(info, unit, q_own, q_other, q_all):
    rows = q_own.shape[2]
    away, home, slot = (unit_info(info, unit, n) for n in range(3))
    for dy in range(2):
        d = home * 2 + dy
        block = jnp.where(away == 1, q_other[d, slot], q_own[d, slot])
        for g in range(GROUP):
            at = (g * 2 + dy) * rows
            q_all[at : at + rows, :] = block[:, g * HEAD : (g + 1) * HEAD]


def online_step(q, k, v, mask, state):
    top, total, mixed = state
    scores = lax.dot_general(k, q, (((1,), (1,)), ((), ())), preferred_element_type=jnp.float32)
    scores = scores * SCORE_FACTOR
    if mask is not None:
        scores = jnp.where(mask, scores, LOWEST)
    new_top = jnp.maximum(top, jnp.max(scores, axis=0, keepdims=True))
    scale = jnp.exp2(top - new_top)
    weights = jnp.exp2(scores - new_top)
    total = total * scale + jnp.sum(weights, axis=0, keepdims=True)
    mixed = mixed * scale + lax.dot_general(
        v, weights.astype(jnp.bfloat16), (((0,), (0,)), ((), ())),
        preferred_element_type=jnp.float32,
    )
    return new_top, total, mixed


def prompt_kernel(layout, slots, chunk, info, q_own, q_other, p_own, p_other, *refs):
    mixed_ref, top_ref, total_ref, k_all, v_all, q_all = refs
    x, core, r, y = info[0], info[1], info[2], info[3]
    rows = p_own.shape[0] // (layout.rings * 4)
    queries = q_all.shape[0]
    for o, piece in enumerate((p_own, p_other)):
        for k in range(layout.rings):
            for d in range(4):
                group = (x ^ (d >> 1)) * 2 + (core ^ o)
                seq = lax.rem(r + layout.rings - k, layout.rings) * 2 + (y ^ (d & 1))
                at = pl.multiple_of((group * layout.rings * 2 + seq) * rows, rows)
                here = (k * 4 + d) * rows
                k_all[pl.ds(at, rows), :] = piece[here : here + rows, :HEAD]
                v_all[pl.ds(at, rows), :] = piece[here : here + rows, HEAD:]
    for n, unit in enumerate(slots):
        length, offset = unit_info(info, unit, 3), unit_info(info, unit, 4)

        @pl.when(r * (queries // GROUP) < length)
        def _():
            load_queries(info, unit, q_own, q_other, q_all)

            def run(step, state, masked):
                at = pl.multiple_of(step * chunk, chunk)
                mask = None
                if masked:
                    place = lax.broadcasted_iota(jnp.int32, (chunk, queries), 0) + at
                    mask = place < offset
                return online_step(
                    q_all[...], k_all[pl.ds(at, chunk), :], v_all[pl.ds(at, chunk), :], mask, state
                )

            state = (
                jnp.full((1, queries), LOWEST, jnp.float32),
                jnp.zeros((1, queries), jnp.float32),
                jnp.zeros((HEAD, queries), jnp.float32),
            )
            whole = offset // chunk
            state = lax.fori_loop(0, whole, lambda i, s: run(i, s, False), state)
            top_ref[n], total_ref[n], mixed_ref[n] = state

            @pl.when(whole * chunk < offset)
            def _():
                state = run(whole, (top_ref[n], total_ref[n], mixed_ref[n]), True)
                top_ref[n], total_ref[n], mixed_ref[n] = state


def response_kernel(layout, w, chunk, info, place_ref, q_own, q_other, mixed, top, total, *refs):
    pieces, outs = refs[: layout.rings], refs[layout.rings : layout.rings + 4]
    k_all, v_all, q_all = refs[layout.rings + 4 :]
    r, y = info[2], info[3]
    rows = outs[0].shape[0]
    queries = q_all.shape[0]
    for dx in range(2):
        unit = w * 2 + dx
        length = unit_info(info, unit, 3)

        @pl.when(r * (2 * rows) >= length)
        def _():
            for dy in range(2):
                outs[dx * 2 + dy][...] = jnp.zeros((rows, WIDE), jnp.bfloat16)

        @pl.when(r * (2 * rows) < length)
        def _():
            load_queries(info, unit, q_own, q_other, q_all)
            for k, piece in enumerate(pieces):
                for dy in range(2):
                    seq = lax.rem(r + layout.rings - k, layout.rings) * 2 + (y ^ dy)
                    at = pl.multiple_of(seq * rows, rows)
                    k_all[pl.ds(at, rows), :] = piece[dx, dy, :, :HEAD]
                    v_all[pl.ds(at, rows), :] = piece[dx, dy, :, HEAD:]
            place = place_ref[...]

            def run(step, state):
                at = pl.multiple_of(step * chunk, chunk)
                key = lax.broadcasted_iota(jnp.int32, (chunk, queries), 0) + at
                mask = key <= jnp.minimum(place, length - 1)
                return online_step(
                    q_all[...], k_all[pl.ds(at, chunk), :], v_all[pl.ds(at, chunk), :], mask, state
                )

            last = jnp.minimum((r + 1) * 2 * rows, length)
            state = (top[dx], total[dx], mixed[dx])
            _, sums, out = lax.fori_loop(0, (last + chunk - 1) // chunk, run, state)
            out = jnp.where(place < length, out / sums, 0.0).T
            for dy in range(2):
                for g in range(GROUP):
                    at = (g * 2 + dy) * rows
                    part = out[at : at + rows].astype(jnp.bfloat16)
                    outs[dx * 2 + dy][:, g * HEAD : (g + 1) * HEAD] = part


def join_kernel(info, *refs):
    pieces, out = refs[:-1], refs[-1]
    own = info[0] * 2 + info[3]
    for w in range(out.shape[0]):
        for d in range(4):
            lane = pl.ds(pl.multiple_of((own ^ d) * WIDE, HEAD), WIDE)
            out[w, :, lane] = pieces[w * 4 + d][...]


def divisor(total, *choices):
    for choice in choices:
        if total % choice == 0:
            return choice
    return total


def struct(*shape, dtype=jnp.bfloat16):
    return jax.ShapeDtypeStruct(shape, dtype)


def device_info(cands, lengths, offsets, ranks):
    group = lax.axis_index("cand").astype(jnp.int32)
    seq = lax.axis_index("seq").astype(jnp.int32)
    x, core = group // 2, group % 2
    every = jnp.arange(ranks.shape[0], dtype=jnp.int32)
    values = [x, core, seq // 2, seq % 2]
    for w in range(cands):
        for dx in range(2):
            rank = ((x ^ dx) * 2 + core) * cands + w
            hit = (ranks == rank).astype(jnp.int32)
            source = jnp.sum(hit * every)
            home = source // cands
            values += [
                (home % 2) ^ core,
                (home // 2) ^ x,
                source % cands,
                jnp.sum(hit * lengths),
                jnp.sum(hit * offsets),
            ]
    return jnp.stack(values)


def body(layout, q, rk, rv, pk, pv, lengths, offsets, ranks):
    cands, rows = q.shape[0], q.shape[1]
    prompt_rows = pk.shape[0]
    queries = 2 * rows * GROUP
    info = device_info(cands, lengths, offsets, ranks)
    bf16 = functools.partial(pltpu.VMEM, dtype=jnp.bfloat16)

    packed = struct(cands * rows + prompt_rows, 2 * HEAD)
    keys = kernel_call(
        pack_keys_kernel, [packed] * 4, (info, rk, rv, pk, pv), name="pack_keys"
    )
    asked = kernel_call(
        pack_queries_kernel, [struct(cands, rows, WIDE)] * 4, (info, q), name="pack_queries"
    )
    keys = jnp.stack(layout.exchange(keys))
    prompt = keys[:, cands * rows :, :].reshape(4 * prompt_rows, 2 * HEAD)
    prompt = jnp.concatenate(layout.ring_gather(prompt), axis=0)
    prompt_other = layout.permute(prompt, core=1)

    keys_other = layout.permute(keys, core=1)
    slots = kernel_call(
        functools.partial(select_keys_kernel, cands, rows),
        [struct(2, 2, rows, 2 * HEAD)] * cands,
        (info, keys, keys_other),
        name="select_keys",
    )
    asked = jnp.stack(layout.exchange(asked))
    asked_other = layout.permute(asked, core=1)
    base = jnp.arange(queries, dtype=jnp.int32)
    seq_of = info[2] * 2 + (info[3] ^ (base // rows % 2))
    place = (seq_of * rows + base % rows)[None, :]

    prompt_keys = 2 * prompt.shape[0]
    chunk = divisor(prompt_keys, 512, 256, 128)
    finished = []
    for w in range(cands):
        units = (w * 2, w * 2 + 1)
        state = kernel_call(
            functools.partial(prompt_kernel, layout, units, chunk),
            [
                struct(2, HEAD, queries, dtype=jnp.float32),
                struct(2, 1, queries, dtype=jnp.float32),
                struct(2, 1, queries, dtype=jnp.float32),
            ],
            (info, asked, asked_other, prompt, prompt_other),
            scratch=[bf16((prompt_keys, HEAD))] * 2 + [bf16((queries, HEAD))],
            cost=(8 * queries * prompt_keys * HEAD, 4 * prompt.size),
            name="prompt_part",
        )
        pieces = layout.ring_gather(slots[w])
        response_keys = layout.rings * 2 * rows
        outs = kernel_call(
            functools.partial(response_kernel, layout, w, divisor(response_keys, 384, 256, 128)),
            [struct(rows, WIDE)] * 4,
            (info, place, asked, asked_other, *state, *pieces),
            scratch=[bf16((response_keys, HEAD))] * 2 + [bf16((queries, HEAD))],
            cost=(8 * queries * response_keys * HEAD, 4 * slots[w].size * layout.rings),
            name="response_part",
        )
        finished += layout.exchange(outs)
    return kernel_call(
        join_kernel, struct(*q.shape), (info, *finished), name="join_heads"
    )


def solution(mesh):
    in_specs = (
        P("cand", "seq", None),
        P("cand", "seq", None),
        P("cand", "seq", None),
        P(("cand", "seq"), None),
        P(("cand", "seq"), None),
        P(),
        P(),
        P(),
    )
    return jax.shard_map(
        functools.partial(body, Layout(mesh)),
        mesh=mesh,
        in_specs=in_specs,
        out_specs=P("cand", "seq", None),
        check_vma=False,
    )
```

time: 306 us -> 131 us (0.43)
  waiting for transfers between devices: 163 us -> 49.9 us
  matrix products: 57.7 us -> 0 us
  Pallas kernels: 0 us -> 40.3 us
  other arithmetic: 29.6 us -> 1.79 us
  local copies, waits for them, and re-layouts: 36.7 us -> 10.2 us
  starting transfers between devices: 0.16 us -> 19.1 us
  between operations: 16.9 us -> 10.3 us
    all_gather x5 -> x0, waiting for transfers between devices: 162 us -> none  [the longest x1 58.4 us: body(): lax.all_gather(prompt_value_array, ('cand', 'seq'), axis=0, tiled=True)]
    dot_general x14 -> x0, matrix products: 57.7 us -> none  [the longest x4 23.1 us: attend_block(): jnp.einsum('chgrn,nhd->chgrd', weights, values_split, preferred_element_t...]
    ppermute x0 -> x24, waiting for transfers between devices: none -> 49.9 us  [permute(): return lax.ppermute(array, AXES, pairs)]
    pallas_call x0 -> x8, Pallas kernels: none -> 40.3 us  [kernel_call(): pl.pallas_call(kernel, out_shape=out_shape, in_specs=[SMEM] + [VMEM] * (l...]
    reduce_sum x8 -> x1, other arithmetic: 23 us -> 0.87 us  [device_info(): jnp.sum(hit * offsets)]
    ppermute x0 -> x24, starting transfers between devices: none -> 19.1 us  [permute(): return lax.ppermute(array, AXES, pairs)]
    dynamic_slice x31 -> x0, local copies, waits for them, and re-layouts: 17.7 us -> none  [the longest x14 13.3 us: one_block(): lax.dynamic_slice_in_dim(all_values, block_start, block_len, keys_axis)]
    while x37 -> x0, local copies, waits for them, and re-layouts: 7.33 us -> none
  transfers between devices with their start and end apart: 5 -> 24, of which waited for: 4 -> 13; matrix products, arithmetic and copies ran while one was open for 25% -> 1% of each run, Pallas kernels for 0% -> 27%
where the time goes in v1:
time: 131 us
  waiting for transfers between devices  49.9 us (38%)
  Pallas kernels  40.3 us (31%)
  starting transfers between devices  19.1 us (15%)
  between operations  10.3 us (8%)
  local copies, waits for them, and re-layouts  10.2 us (8%)
  other arithmetic  1.79 us (1%)
    ppermute x24, waiting for transfers between devices, permute(): return lax.ppermute(array, AXES, pairs)  49.9 us
    pallas_call x8, Pallas kernels, kernel_call(): pl.pallas_call(kernel, out_shape=out_shape, in_specs=[SMEM] + [VMEM] * (l...  40.3 us
    ppermute x24, starting transfers between devices, permute(): return lax.ppermute(array, AXES, pairs)  19.1 us
    another operation x1, local copies, waits for them, and re-layouts, device_info(): return jnp.stack(values)  5.57 us
    unnamed x48, local copies, waits for them, and re-layouts  4.63 us
  transfers between devices with their start and end apart: 24, of which 13 were waited for; matrix products, arithmetic and copies ran while one was open for 1% of the time, Pallas kernels for 27%

profile of v1, /device:TPU:0, one launch (start us, length us, event | category | flops | bytes accessed | tf_op | source)
XLA Modules:
  0.0 131.5 jit_solution(4751919047369397815)
XLA Ops:
  11.6 5.6 %stack.129.info = s32[24]{0:T(128)} concatenate(s32[1]{0:T(128)} %bitcast, s32[1]{0:T(128)} %bitcast.1, s32[1]{0:T(128)} %bitcast.2, s32[1]{0:T(128)} %bitcast.3, s32[1]{0:T(128)} %bitcast.4, s32[1]{0:T(128)} %bitcast.5, s32[1]{0:T(128)} %bitcast.6, s32[1]{0:T(128)} %bitcast.7, s32[1]{0:T(128)} %bitcast.8, s32[1]{0:T(128)} %bitcast.9, s32[1]{0:T(128)} %bitcast.10, s32[1]{0:T(128)} %bitcast.11, ...), dimensions={0} | concatenate | bytes 192 | tf_op jit(solution)/shard_map/stack | solution.py:263
  17.1 2.0 %pack_keys.1 = (bf16[256,256]{1,0:T(8,128)(2,1)}, bf16[256,256]{1,0:T(8,128)(2,1)}, bf16[256,256]{1,0:T(8,128)(2,1)}, bf16[256,256]{1,0:T(8,128)(2,1)}) custom-call(s32[24]{0:T(128)} %stack.129.info, bf16[2,96,512]{2,1,0:T(8,128)(2,1)} %rk.1, bf16[2,96,512]{2,1,0:T(8,128)(2,1)} %rv.1, bf16[64,512]{1,0:T(8,128)(2,1)} %pk.1, bf16[64,512]{1,0:T(8,128)(2,1)} %pv.1), custom_call_target="tpu_custom_call" | custom-call | tf_op jit(solution)/shard_map/pack_keys/pallas_call | solution.py:55
  19.1 3.0 %collective-permute-start.4 = (bf16[256,256]{1,0:T(8,128)(2,1)}, bf16[256,256]{1,0:T(8,128)(2,1)S(1)}, u32[]{:S(2)}, u32[]{:S(2)}) collective-permute-start(bf16[256,256]{1,0:T(8,128)(2,1)} %get-tuple-element.34), channel_id=1, source_target_pairs={{0,1},{1,0},{2,3},{3,2},{4,5},{5,4},{6,7},{7,6},{8,9},{9,8},{10,11... | collective-permute-start | bytes 393224 | tf_op jit(solution)/shard_map/ppermute | solution.py:41
  23.6 2.3 %pack_queries.1 = (bf16[2,96,640]{2,1,0:T(8,128)(2,1)}, bf16[2,96,640]{2,1,0:T(8,128)(2,1)}, bf16[2,96,640]{2,1,0:T(8,128)(2,1)}, bf16[2,96,640]{2,1,0:T(8,128)(2,1)}) custom-call(s32[24]{0:T(128)} %stack.129.info, bf16[2,96,2560]{2,1,0:T(8,128)(2,1)} %q.1), custom_call_target="tpu_custom_call" | custom-call | tf_op jit(solution)/shard_map/pack_queries/pallas_call | solution.py:55
  25.9 2.0 %collective-permute-start = (bf16[2,96,640]{2,1,0:T(8,128)(2,1)}, bf16[2,96,640]{2,1,0:T(8,128)(2,1)S(1)}, u32[]{:S(2)}, u32[]{:S(2)}) collective-permute-start(bf16[2,96,640]{2,1,0:T(8,128)(2,1)} %get-tuple-element.30), channel_id=1, source_target_pairs={{0,1},{1,0},{2,3},{3,2},{4,5},{5,4},{6,7},{7,6},{8,9},{9,8},{10,11... | collective-permute-start | bytes 737288 | tf_op jit(solution)/shard_map/ppermute | solution.py:41
  27.8 1.5 %collective-permute-start.1 = (bf16[2,96,640]{2,1,0:T(8,128)(2,1)}, bf16[2,96,640]{2,1,0:T(8,128)(2,1)S(1)}, u32[]{:S(2)}, u32[]{:S(2)}) collective-permute-start(bf16[2,96,640]{2,1,0:T(8,128)(2,1)} %get-tuple-element.31), channel_id=1, source_target_pairs={{0,16},{1,17},{2,18},{3,19},{4,20},{5,21},{6,22},{7,23},{8,24},{9,... | collective-permute-start | bytes 737288 | tf_op jit(solution)/shard_map/ppermute | solution.py:41
  30.7 1.9 %collective-permute-start.7 = (bf16[256,256]{1,0:T(8,128)(2,1)S(1)}, bf16[256,256]{1,0:T(8,128)(2,1)S(1)}, u32[]{:S(2)}, u32[]{:S(2)}) collective-permute-start(bf16[256,256]{1,0:T(8,128)(2,1)S(1)} %bitcast.33), channel_id=1, source_target_pairs={{0,2},{1,3},{2,4},{3,5},{4,6},{5,7},{6,0},{7,1},{8,10},{9,11},{10,... | collective-permute-start | bytes 393224 | tf_op jit(solution)/shard_map/ppermute | solution.py:41
  32.6 3.9 %collective-permute-done = bf16[2,96,640]{2,1,0:T(8,128)(2,1)S(1)} collective-permute-done((bf16[2,96,640]{2,1,0:T(8,128)(2,1)}, bf16[2,96,640]{2,1,0:T(8,128)(2,1)S(1)}, u32[]{:S(2)}, u32[]{:S(2)}) %collective-permute-start) | collective-permute-done | bytes 245792 | tf_op jit(solution)/shard_map/ppermute | solution.py:41
  36.9 3.4 %collective-permute-done.2 = bf16[2,96,640]{2,1,0:T(8,128)(2,1)S(1)} collective-permute-done((bf16[2,96,640]{2,1,0:T(8,128)(2,1)}, bf16[2,96,640]{2,1,0:T(8,128)(2,1)S(1)}, u32[]{:S(2)}, u32[]{:S(2)}) %collective-permute-start.2) | collective-permute-done | bytes 245792 | tf_op jit(solution)/shard_map/ppermute | solution.py:41
  40.6 1.9 %collective-permute-start.8 = (bf16[256,256]{1,0:T(8,128)(2,1)S(1)}, bf16[256,256]{1,0:T(8,128)(2,1)S(1)}, u32[]{:S(2)}, u32[]{:S(2)}) collective-permute-start(bf16[256,256]{1,0:T(8,128)(2,1)S(1)} %collective-permute-done.7), channel_id=1, source_target_pairs={{0,2},{1,3},{2,4},{3,5},{4,6},{5,7},{6,0},{7,1},{8,10},{9,11},{10,... | collective-permute-start | bytes 393224 | tf_op jit(solution)/shard_map/ppermute | solution.py:41
  42.4 6.1 %collective-permute-done.8 = bf16[256,256]{1,0:T(8,128)(2,1)S(1)} collective-permute-done((bf16[256,256]{1,0:T(8,128)(2,1)S(1)}, bf16[256,256]{1,0:T(8,128)(2,1)S(1)}, u32[]{:S(2)}, u32[]{:S(2)}) %collective-permute-start.8) | collective-permute-done | bytes 131104 | tf_op jit(solution)/shard_map/ppermute | solution.py:41
  48.6 7.1 %collective-permute-done.9 = bf16[256,256]{1,0:T(8,128)(2,1)S(1)} collective-permute-done((bf16[256,256]{1,0:T(8,128)(2,1)S(1)}, bf16[256,256]{1,0:T(8,128)(2,1)S(1)}, u32[]{:S(2)}, u32[]{:S(2)}) %collective-permute-start.9) | collective-permute-done | bytes 131104 | tf_op jit(solution)/shard_map/ppermute | solution.py:41
  56.7 2.0 %select_keys.1 = (bf16[2,2,96,256]{3,2,1,0:T(8,128)(2,1)}, bf16[2,2,96,256]{3,2,1,0:T(8,128)(2,1)}) custom-call(s32[24]{0:T(128)} %stack.129.info, bf16[4,256,256]{2,1,0:T(8,128)(2,1)} %copy-done.2, bf16[4,256,256]{2,1,0:T(8,128)(2,1)} %copy-done.4), custom_call_target="tpu_custom_call" | custom-call | tf_op jit(solution)/shard_map/select_keys/pallas_call | solution.py:55
  58.8 9.7 %collective-permute-done.18.refs_1_ = bf16[2,2,96,256]{3,2,1,0:T(8,128)(2,1)S(1)} collective-permute-done((bf16[2,2,96,256]{3,2,1,0:T(8,128)(2,1)}, bf16[2,2,96,256]{3,2,1,0:T(8,128)(2,1)S(1)}, u32[]{:S(2)}, u32[]{:S(2)}) %collective-permute-start.18) | collective-permute-done | bytes 196640 | tf_op jit(solution)/shard_map/ppermute | solution.py:41
  68.5 3.9 %collective-permute-done.12.refs_1_ = bf16[2,2,96,256]{3,2,1,0:T(8,128)(2,1)S(1)} collective-permute-done((bf16[2,2,96,256]{3,2,1,0:T(8,128)(2,1)}, bf16[2,2,96,256]{3,2,1,0:T(8,128)(2,1)S(1)}, u32[]{:S(2)}, u32[]{:S(2)}) %collective-permute-start.12) | collective-permute-done | bytes 196640 | tf_op jit(solution)/shard_map/ppermute | solution.py:41
  72.3 4.2 %collective-permute-done.19.refs_2_ = bf16[2,2,96,256]{3,2,1,0:T(8,128)(2,1)S(1)} collective-permute-done((bf16[2,2,96,256]{3,2,1,0:T(8,128)(2,1)S(1)}, bf16[2,2,96,256]{3,2,1,0:T(8,128)(2,1)S(1)}, u32[]{:S(2)}, u32[]{:S(2)}) %collective-permute-start.19) | collective-permute-done | bytes 196640 | tf_op jit(solution)/shard_map/ppermute | solution.py:41
  77.2 4.8 %collective-permute-done.13.refs_2_ = bf16[2,2,96,256]{3,2,1,0:T(8,128)(2,1)S(1)} collective-permute-done((bf16[2,2,96,256]{3,2,1,0:T(8,128)(2,1)S(1)}, bf16[2,2,96,256]{3,2,1,0:T(8,128)(2,1)S(1)}, u32[]{:S(2)}, u32[]{:S(2)}) %collective-permute-start.13) | collective-permute-done | bytes 196640 | tf_op jit(solution)/shard_map/ppermute | solution.py:41
  83.0 10.1 %prompt_part.3 = (f32[2,128,960]{2,1,0:T(8,128)}, f32[2,1,960]{2,1,0:T(1,128)}, f32[2,1,960]{2,1,0:T(1,128)}) custom-call(s32[24]{0:T(128)} %stack.129.info, bf16[4,2,96,640]{3,2,1,0:T(8,128)(2,1)} %copy-done, bf16[4,2,96,640]{3,2,1,0:T(8,128)(2,1)} %copy-done.1, bf16[1024,256]{1,0:T(8,128)(2,1)} %copy-done.3, bf16[1024,256]{1,0:T(8,128)(2,1)} %collective-permute-done.10.p_other), custom_call_target="tpu_custom_call" | custom-call | flops 2013265920 | bytes 1048576 | tf_op jit(solution)/shard_map/prompt_part/pallas_call | solution.py:55
  93.8 5.7 %response_part.3 = (bf16[96,640]{1,0:T(8,128)(2,1)}, bf16[96,640]{1,0:T(8,128)(2,1)}, bf16[96,640]{1,0:T(8,128)(2,1)}, bf16[96,640]{1,0:T(8,128)(2,1)}) custom-call(s32[24]{0:T(128)} %stack.129.info, s32[1,960]{1,0:T(1,128)} %fusion.place_ref, bf16[4,2,96,640]{3,2,1,0:T(8,128)(2,1)} %copy-done, bf16[4,2,96,640]{3,2,1,0:T(8,128)(2,1)} %copy-done.1, ...), custom_call_target="tpu_custom_call" | custom-call | flops 754974720 | bytes 1572864 | tf_op jit(solution)/shard_map/response_part/pallas_call | solution.py:55
  101.0 10.2 %prompt_part.2 = (f32[2,128,960]{2,1,0:T(8,128)}, f32[2,1,960]{2,1,0:T(1,128)}, f32[2,1,960]{2,1,0:T(1,128)}) custom-call(s32[24]{0:T(128)} %stack.129.info, bf16[4,2,96,640]{3,2,1,0:T(8,128)(2,1)} %copy-done, bf16[4,2,96,640]{3,2,1,0:T(8,128)(2,1)} %copy-done.1, bf16[1024,256]{1,0:T(8,128)(2,1)} %copy-done.3, bf16[1024,256]{1,0:T(8,128)(2,1)} %collective-permute-done.10.p_other), custom_call_target="tpu_custom_call" | custom-call | flops 2013265920 | bytes 1048576 | tf_op jit(solution)/shard_map/prompt_part/pallas_call | solution.py:55
  114.0 5.7 %response_part.2 = (bf16[96,640]{1,0:T(8,128)(2,1)}, bf16[96,640]{1,0:T(8,128)(2,1)}, bf16[96,640]{1,0:T(8,128)(2,1)}, bf16[96,640]{1,0:T(8,128)(2,1)}) custom-call(s32[24]{0:T(128)} %stack.129.info, s32[1,960]{1,0:T(1,128)} %fusion.place_ref, bf16[4,2,96,640]{3,2,1,0:T(8,128)(2,1)} %copy-done, bf16[4,2,96,640]{3,2,1,0:T(8,128)(2,1)} %copy-done.1, ...), custom_call_target="tpu_custom_call" | custom-call | flops 754974720 | bytes 1572864 | tf_op jit(solution)/shard_map/response_part/pallas_call | solution.py:55
  123.2 1.6 %collective-permute-done.15.refs_1_ = bf16[96,640]{1,0:T(8,128)(2,1)S(1)} collective-permute-done((bf16[96,640]{1,0:T(8,128)(2,1)}, bf16[96,640]{1,0:T(8,128)(2,1)S(1)}, u32[]{:S(2)}, u32[]{:S(2)}) %collective-permute-start.15) | collective-permute-done | bytes 122912 | tf_op jit(solution)/shard_map/ppermute | solution.py:41
  126.1 2.4 %collective-permute-done.17.refs_3_ = bf16[96,640]{1,0:T(8,128)(2,1)S(1)} collective-permute-done((bf16[96,640]{1,0:T(8,128)(2,1)}, bf16[96,640]{1,0:T(8,128)(2,1)S(1)}, u32[]{:S(2)}, u32[]{:S(2)}) %collective-permute-start.17) | collective-permute-done | bytes 122912 | tf_op jit(solution)/shard_map/ppermute | solution.py:41
  129.2 2.3 %join_heads.1 = bf16[2,96,2560]{2,1,0:T(8,128)(2,1)} custom-call(s32[24]{0:T(128)} %stack.129.info, bf16[96,640]{1,0:T(8,128)(2,1)} %get-tuple-element.41.refs_0_, bf16[96,640]{1,0:T(8,128)(2,1)} %copy-done.16, bf16[96,640]{1,0:T(8,128)(2,1)} %copy-done.17, bf16[96,640]{1,0:T(8,128)(2,1)} %copy-done.18, bf16[96,640]{1,0:T(8,128)(2,1)} %get-tuple-element.49.refs_4_, ...), custom_call_target="tpu_custom_call" | custom-call | tf_op jit(solution)/shard_map/join_heads/pallas_call | solution.py:55
  (87 shorter events, 18.3 us)
Async XLA Ops:
  19.1 10.2 %collective-permute-start.4 = (bf16[256,256]{1,0:T(8,128)(2,1)}, bf16[256,256]{1,0:T(8,128)(2,1)S(1)}, u32[]{:S(2)}, u32[]{:S(2)}) collective-permute-start(bf16[256,256]{1,0:T(8,128)(2,1)} %get-tuple-element.34), channel_id=1, source_target_pairs={{0,1},{1,0},{2,3},{3,2},{4,5},{5,4},{6,7},{7,6},{8,9},{9,8},{10,11... | collective-permute-start | bytes 393224 | tf_op jit(solution)/shard_map/ppermute | solution.py:41
  22.1 7.3 %collective-permute-start.5 = (bf16[256,256]{1,0:T(8,128)(2,1)}, bf16[256,256]{1,0:T(8,128)(2,1)S(1)}, u32[]{:S(2)}, u32[]{:S(2)}) collective-permute-start(bf16[256,256]{1,0:T(8,128)(2,1)} %get-tuple-element.35), channel_id=1, source_target_pairs={{0,16},{1,17},{2,18},{3,19},{4,20},{5,21},{6,22},{7,23},{8,24},{9,... | collective-permute-start | bytes 393224 | tf_op jit(solution)/shard_map/ppermute | solution.py:41
  23.6 6.9 %collective-permute-start.6 = (bf16[256,256]{1,0:T(8,128)(2,1)}, bf16[256,256]{1,0:T(8,128)(2,1)S(1)}, u32[]{:S(2)}, u32[]{:S(2)}) collective-permute-start(bf16[256,256]{1,0:T(8,128)(2,1)} %get-tuple-element.36), channel_id=1, source_target_pairs={{0,17},{1,16},{2,19},{3,18},{4,21},{5,20},{6,23},{7,22},{8,25},{9,... | collective-permute-start | bytes 393224 | tf_op jit(solution)/shard_map/ppermute | solution.py:41
  25.9 10.6 %collective-permute-start = (bf16[2,96,640]{2,1,0:T(8,128)(2,1)}, bf16[2,96,640]{2,1,0:T(8,128)(2,1)S(1)}, u32[]{:S(2)}, u32[]{:S(2)}) collective-permute-start(bf16[2,96,640]{2,1,0:T(8,128)(2,1)} %get-tuple-element.30), channel_id=1, source_target_pairs={{0,1},{1,0},{2,3},{3,2},{4,5},{5,4},{6,7},{7,6},{8,9},{9,8},{10,11... | collective-permute-start | bytes 737288 | tf_op jit(solution)/shard_map/ppermute | solution.py:41
  27.8 9.1 %collective-permute-start.1 = (bf16[2,96,640]{2,1,0:T(8,128)(2,1)}, bf16[2,96,640]{2,1,0:T(8,128)(2,1)S(1)}, u32[]{:S(2)}, u32[]{:S(2)}) collective-permute-start(bf16[2,96,640]{2,1,0:T(8,128)(2,1)} %get-tuple-element.31), channel_id=1, source_target_pairs={{0,16},{1,17},{2,18},{3,19},{4,20},{5,21},{6,22},{7,23},{8,24},{9,... | collective-permute-start | bytes 737288 | tf_op jit(solution)/shard_map/ppermute | solution.py:41
  29.3 11.0 %collective-permute-start.2 = (bf16[2,96,640]{2,1,0:T(8,128)(2,1)}, bf16[2,96,640]{2,1,0:T(8,128)(2,1)S(1)}, u32[]{:S(2)}, u32[]{:S(2)}) collective-permute-start(bf16[2,96,640]{2,1,0:T(8,128)(2,1)} %get-tuple-element.32), channel_id=1, source_target_pairs={{0,17},{1,16},{2,19},{3,18},{4,21},{5,20},{6,23},{7,22},{8,25},{9,... | collective-permute-start | bytes 737288 | tf_op jit(solution)/shard_map/ppermute | solution.py:41
  30.6 25.2 %collective-permute-start.11 = (bf16[4,256,256]{2,1,0:T(8,128)(2,1)S(1)}, bf16[4,256,256]{2,1,0:T(8,128)(2,1)S(1)}, u32[]{:S(2)}, u32[]{:S(2)}) collective-permute-start(bf16[4,256,256]{2,1,0:T(8,128)(2,1)S(1)} %pad_maximum_fusion.1.own), channel_id=1, source_target_pairs={{0,8},{1,9},{2,10},{3,11},{4,12},{5,13},{6,14},{7,15},{8,0},{9,1},... | collective-permute-start | bytes 1572872 | tf_op jit(solution)/shard_map/ppermute | solution.py:41
  30.7 9.9 %collective-permute-start.7 = (bf16[256,256]{1,0:T(8,128)(2,1)S(1)}, bf16[256,256]{1,0:T(8,128)(2,1)S(1)}, u32[]{:S(2)}, u32[]{:S(2)}) collective-permute-start(bf16[256,256]{1,0:T(8,128)(2,1)S(1)} %bitcast.33), channel_id=1, source_target_pairs={{0,2},{1,3},{2,4},{3,5},{4,6},{5,7},{6,0},{7,1},{8,10},{9,11},{10,... | collective-permute-start | bytes 393224 | tf_op jit(solution)/shard_map/ppermute | solution.py:41
  40.5 41.5 %collective-permute-start.3 = (bf16[4,2,96,640]{3,2,1,0:T(8,128)(2,1)S(1)}, bf16[4,2,96,640]{3,2,1,0:T(8,128)(2,1)S(1)}, u32[]{:S(2)}, u32[]{:S(2)}) collective-permute-start(bf16[4,2,96,640]{3,2,1,0:T(8,128)(2,1)S(1)} %pad_maximum_fusion.q_own), channel_id=1, source_target_pairs={{0,8},{1,9},{2,10},{3,11},{4,12},{5,13},{6,14},{7,15},{8,0},{9,1},... | collective-permute-start | bytes 2949128 | tf_op jit(solution)/shard_map/ppermute | solution.py:41
  40.6 8.0 %collective-permute-start.8 = (bf16[256,256]{1,0:T(8,128)(2,1)S(1)}, bf16[256,256]{1,0:T(8,128)(2,1)S(1)}, u32[]{:S(2)}, u32[]{:S(2)}) collective-permute-start(bf16[256,256]{1,0:T(8,128)(2,1)S(1)} %collective-permute-done.7), channel_id=1, source_target_pairs={{0,2},{1,3},{2,4},{3,5},{4,6},{5,7},{6,0},{7,1},{8,10},{9,11},{10,... | collective-permute-start | bytes 393224 | tf_op jit(solution)/shard_map/ppermute | solution.py:41
  48.6 7.1 %collective-permute-start.9 = (bf16[256,256]{1,0:T(8,128)(2,1)S(1)}, bf16[256,256]{1,0:T(8,128)(2,1)S(1)}, u32[]{:S(2)}, u32[]{:S(2)}) collective-permute-start(bf16[256,256]{1,0:T(8,128)(2,1)S(1)} %collective-permute-done.8), channel_id=1, source_target_pairs={{0,2},{1,3},{2,4},{3,5},{4,6},{5,7},{6,0},{7,1},{8,10},{9,11},{10,... | collective-permute-start | bytes 393224 | tf_op jit(solution)/shard_map/ppermute | solution.py:41
  55.7 26.3 %collective-permute-start.10 = (bf16[1024,256]{1,0:T(8,128)(2,1)S(1)}, bf16[1024,256]{1,0:T(8,128)(2,1)}, u32[]{:S(2)}, u32[]{:S(2)}) collective-permute-start(bf16[1024,256]{1,0:T(8,128)(2,1)S(1)} %pad_maximum_fusion.2.p_own), channel_id=1, source_target_pairs={{0,8},{1,9},{2,10},{3,11},{4,12},{5,13},{6,14},{7,15},{8,0},{9,1},... | collective-permute-start | bytes 1572872 | tf_op jit(solution)/shard_map/ppermute | solution.py:41
  58.7 9.8 %collective-permute-start.18 = (bf16[2,2,96,256]{3,2,1,0:T(8,128)(2,1)}, bf16[2,2,96,256]{3,2,1,0:T(8,128)(2,1)S(1)}, u32[]{:S(2)}, u32[]{:S(2)}) collective-permute-start(bf16[2,2,96,256]{3,2,1,0:T(8,128)(2,1)} %get-tuple-element.48.refs_0_), channel_id=1, source_target_pairs={{0,2},{1,3},{2,4},{3,5},{4,6},{5,7},{6,0},{7,1},{8,10},{9,11},{10,... | collective-permute-start | bytes 589832 | tf_op jit(solution)/shard_map/ppermute | solution.py:41
  58.7 13.6 %collective-permute-start.12 = (bf16[2,2,96,256]{3,2,1,0:T(8,128)(2,1)}, bf16[2,2,96,256]{3,2,1,0:T(8,128)(2,1)S(1)}, u32[]{:S(2)}, u32[]{:S(2)}) collective-permute-start(bf16[2,2,96,256]{3,2,1,0:T(8,128)(2,1)} %get-tuple-element.40.refs_0_), channel_id=1, source_target_pairs={{0,2},{1,3},{2,4},{3,5},{4,6},{5,7},{6,0},{7,1},{8,10},{9,11},{10,... | collective-permute-start | bytes 589832 | tf_op jit(solution)/shard_map/ppermute | solution.py:41
  68.5 8.1 %collective-permute-start.19 = (bf16[2,2,96,256]{3,2,1,0:T(8,128)(2,1)S(1)}, bf16[2,2,96,256]{3,2,1,0:T(8,128)(2,1)S(1)}, u32[]{:S(2)}, u32[]{:S(2)}) collective-permute-start(bf16[2,2,96,256]{3,2,1,0:T(8,128)(2,1)S(1)} %collective-permute-done.18.refs_1_), channel_id=1, source_target_pairs={{0,2},{1,3},{2,4},{3,5},{4,6},{5,7},{6,0},{7,1},{8,10},{9,11},{10,... | collective-permute-start | bytes 589832 | tf_op jit(solution)/shard_map/ppermute | solution.py:41
  72.3 9.6 %collective-permute-start.13 = (bf16[2,2,96,256]{3,2,1,0:T(8,128)(2,1)S(1)}, bf16[2,2,96,256]{3,2,1,0:T(8,128)(2,1)S(1)}, u32[]{:S(2)}, u32[]{:S(2)}) collective-permute-start(bf16[2,2,96,256]{3,2,1,0:T(8,128)(2,1)S(1)} %collective-permute-done.12.refs_1_), channel_id=1, source_target_pairs={{0,2},{1,3},{2,4},{3,5},{4,6},{5,7},{6,0},{7,1},{8,10},{9,11},{10,... | collective-permute-start | bytes 589832 | tf_op jit(solution)/shard_map/ppermute | solution.py:41
  76.5 16.6 %collective-permute-start.20 = (bf16[2,2,96,256]{3,2,1,0:T(8,128)(2,1)S(1)}, bf16[2,2,96,256]{3,2,1,0:T(8,128)(2,1)S(1)}, u32[]{:S(2)}, u32[]{:S(2)}) collective-permute-start(bf16[2,2,96,256]{3,2,1,0:T(8,128)(2,1)S(1)} %collective-permute-done.19.refs_2_), channel_id=1, source_target_pairs={{0,2},{1,3},{2,4},{3,5},{4,6},{5,7},{6,0},{7,1},{8,10},{9,11},{10,... | collective-permute-start | bytes 589832 | tf_op jit(solution)/shard_map/ppermute | solution.py:41
  82.0 31.3 %collective-permute-start.14 = (bf16[2,2,96,256]{3,2,1,0:T(8,128)(2,1)S(1)}, bf16[2,2,96,256]{3,2,1,0:T(8,128)(2,1)S(1)}, u32[]{:S(2)}, u32[]{:S(2)}) collective-permute-start(bf16[2,2,96,256]{3,2,1,0:T(8,128)(2,1)S(1)} %collective-permute-done.13.refs_2_), channel_id=1, source_target_pairs={{0,2},{1,3},{2,4},{3,5},{4,6},{5,7},{6,0},{7,1},{8,10},{9,11},{10,... | collective-permute-start | bytes 589832 | tf_op jit(solution)/shard_map/ppermute | solution.py:41
  99.5 23.0 %collective-permute-start.21 = (bf16[96,640]{1,0:T(8,128)(2,1)}, bf16[96,640]{1,0:T(8,128)(2,1)S(1)}, u32[]{:S(2)}, u32[]{:S(2)}) collective-permute-start(bf16[96,640]{1,0:T(8,128)(2,1)} %get-tuple-element.50), channel_id=1, source_target_pairs={{0,1},{1,0},{2,3},{3,2},{4,5},{5,4},{6,7},{7,6},{8,9},{9,8},{10,11... | collective-permute-start | bytes 368648 | tf_op jit(solution)/shard_map/ppermute | solution.py:41
  111.2 12.0 %collective-permute-start.22 = (bf16[96,640]{1,0:T(8,128)(2,1)S(1)}, bf16[96,640]{1,0:T(8,128)(2,1)S(1)}, u32[]{:S(2)}, u32[]{:S(2)}) collective-permute-start(bf16[96,640]{1,0:T(8,128)(2,1)S(1)} %copy-done.23), channel_id=1, source_target_pairs={{0,16},{1,17},{2,18},{3,19},{4,20},{5,21},{6,22},{7,23},{8,24},{9,... | collective-permute-start | bytes 368648 | tf_op jit(solution)/shard_map/ppermute | solution.py:41
  112.7 10.5 %collective-permute-start.23 = (bf16[96,640]{1,0:T(8,128)(2,1)S(1)}, bf16[96,640]{1,0:T(8,128)(2,1)S(1)}, u32[]{:S(2)}, u32[]{:S(2)}) collective-permute-start(bf16[96,640]{1,0:T(8,128)(2,1)S(1)} %copy-done.22), channel_id=1, source_target_pairs={{0,17},{1,16},{2,19},{3,18},{4,21},{5,20},{6,23},{7,22},{8,25},{9,... | collective-permute-start | bytes 368648 | tf_op jit(solution)/shard_map/ppermute | solution.py:41
  119.7 5.1 %collective-permute-start.15 = (bf16[96,640]{1,0:T(8,128)(2,1)}, bf16[96,640]{1,0:T(8,128)(2,1)S(1)}, u32[]{:S(2)}, u32[]{:S(2)}) collective-permute-start(bf16[96,640]{1,0:T(8,128)(2,1)} %get-tuple-element.42), channel_id=1, source_target_pairs={{0,1},{1,0},{2,3},{3,2},{4,5},{5,4},{6,7},{7,6},{8,9},{9,8},{10,11... | collective-permute-start | bytes 368648 | tf_op jit(solution)/shard_map/ppermute | solution.py:41
  121.0 5.1 %collective-permute-start.16 = (bf16[96,640]{1,0:T(8,128)(2,1)}, bf16[96,640]{1,0:T(8,128)(2,1)S(1)}, u32[]{:S(2)}, u32[]{:S(2)}) collective-permute-start(bf16[96,640]{1,0:T(8,128)(2,1)} %get-tuple-element.43), channel_id=1, source_target_pairs={{0,16},{1,17},{2,18},{3,19},{4,20},{5,21},{6,22},{7,23},{8,24},{9,... | collective-permute-start | bytes 368648 | tf_op jit(solution)/shard_map/ppermute | solution.py:41
  122.5 6.0 %collective-permute-start.17 = (bf16[96,640]{1,0:T(8,128)(2,1)}, bf16[96,640]{1,0:T(8,128)(2,1)S(1)}, u32[]{:S(2)}, u32[]{:S(2)}) collective-permute-start(bf16[96,640]{1,0:T(8,128)(2,1)} %get-tuple-element.44), channel_id=1, source_target_pairs={{0,17},{1,16},{2,19},{3,18},{4,21},{5,20},{6,23},{7,22},{8,25},{9,... | collective-permute-start | bytes 368648 | tf_op jit(solution)/shard_map/ppermute | solution.py:41
  (24 other events, 174.5 us)

commit v2 on v1

v2 whole, which is shorter than its diff:
```python
import functools
import math

import jax
import jax.numpy as jnp
from jax import lax
from jax.experimental import pallas as pl
from jax.experimental.pallas import tpu as pltpu
from jax.sharding import PartitionSpec as P

QUERY_HEADS = 20
KEY_VALUE_HEADS = 4
HEAD = 128
GROUP = QUERY_HEADS // KEY_VALUE_HEADS
WIDE = GROUP * HEAD
SCORE_FACTOR = math.log2(math.e) / math.sqrt(HEAD)
LOWEST = -1e30
AXES = ("cand", "seq")
VMEM = pl.BlockSpec(memory_space=pltpu.VMEM)
SMEM = pl.BlockSpec(memory_space=pltpu.SMEM)

FIELDS = 5


class Layout:
    def __init__(self, mesh):
        assert mesh.shape["cand"] == 4 and mesh.shape["seq"] % 2 == 0
        self.rings = mesh.shape["seq"] // 2

    def permute(self, array, d=0, core=0, ring=0):
        pairs = []
        for x in range(2):
            for c in range(2):
                for r in range(self.rings):
                    for y in range(2):
                        source = ((x * 2 + c) * self.rings + r) * 2 + y
                        target = ((x ^ (d >> 1)) * 2 + (c ^ core)) * self.rings
                        target = (target + (r + ring) % self.rings) * 2 + (y ^ (d & 1))
                        pairs.append((source, target))
        return lax.ppermute(array, AXES, pairs)

    def exchange(self, pieces):
        return [pieces[0]] + [self.permute(pieces[d], d=d) for d in range(1, 4)]

    def ring_gather(self, block):
        return [block] + [self.permute(block, ring=k) for k in range(1, self.rings)]


def kernel_call(kernel, out_shape, operands, scratch=(), cost=(0, 0), name=None, scalars=1, spare=2 << 20):
    many = isinstance(out_shape, list)
    arrays = list(operands) + (list(out_shape) if many else [out_shape]) + list(scratch)
    held = sum(math.prod(a.shape) * jnp.dtype(a.dtype).itemsize for a in arrays)
    return pl.pallas_call(
        kernel,
        out_shape=out_shape,
        in_specs=[SMEM] * scalars + [VMEM] * (len(operands) - scalars),
        out_specs=[VMEM] * len(out_shape) if many else VMEM,
        scratch_shapes=list(scratch),
        compiler_params=pltpu.CompilerParams(vmem_limit_bytes=held + held // 4 + spare),
        cost_estimate=pl.CostEstimate(
            flops=cost[0], transcendentals=cost[0] // 512, bytes_accessed=cost[1]
        ),
        name=name,
    )(*operands)


def plan_kernel(cands, lengths, offsets, ranks, info):
    group, seq = lax.axis_index("cand"), lax.axis_index("seq")
    x, core = group // 2, group % 2
    info[0], info[1], info[2], info[3] = x, core, seq // 2, seq % 2
    for w in range(cands):
        for dx in range(2):
            rank = ((x ^ dx) * 2 + core) * cands + w
            source, length, offset = jnp.int32(0), jnp.int32(0), jnp.int32(0)
            for c in range(ranks.shape[0]):
                hit = ranks[c] == rank
                source = jnp.where(hit, c, source)
                length = jnp.where(hit, lengths[c], length)
                offset = jnp.where(hit, offsets[c], offset)
            home = source // cands
            at = 4 + (w * 2 + dx) * FIELDS
            info[at] = (home % 2) ^ core
            info[at + 1] = (home // 2) ^ x
            info[at + 2] = source % cands
            info[at + 3] = length
            info[at + 4] = offset


def own_head():
    return lax.axis_index("cand") // 2 * 2 + lax.axis_index("seq") % 2


def pack_keys_kernel(rk, rv, *outs):
    own = own_head()
    for d, out in enumerate(outs):
        lane = pl.ds(pl.multiple_of((own ^ d) * HEAD, HEAD), HEAD)
        out[:, :, :HEAD] = rk[:, :, lane]
        out[:, :, HEAD:] = rv[:, :, lane]


def pack_prompt_kernel(rings, *refs):
    pieces, outs = refs[:rings], refs[rings:]
    own = own_head()
    rows, width = pieces[0].shape
    for d, out in enumerate(outs):
        lane = pl.multiple_of((own ^ d) * HEAD, HEAD)
        for k, piece in enumerate(pieces):
            out[k * rows : (k + 1) * rows, :HEAD] = piece[:, pl.ds(lane, HEAD)]
            out[k * rows : (k + 1) * rows, HEAD:] = piece[:, pl.ds(lane + width // 2, HEAD)]


def pack_queries_kernel(q, *outs):
    own = own_head()
    for d, out in enumerate(outs):
        lane = pl.ds(pl.multiple_of((own ^ d) * WIDE, HEAD), WIDE)
        for w in range(q.shape[0]):
            out[w] = q[w, :, lane]


def unit_info(info, unit, field):
    return info[4 + unit * FIELDS + field]


def fetch(info, unit, dy, pieces):
    away, home, slot = (unit_info(info, unit, n) for n in range(3))
    near = jnp.where(home == 1, pieces[2 + dy][slot], pieces[dy][slot])
    far = jnp.where(home == 1, pieces[6 + dy][slot], pieces[4 + dy][slot])
    return jnp.where(away == 1, far, near)


def select_keys_kernel(info, *refs):
    pieces, outs = refs[:8], refs[8:]
    for w, out in enumerate(outs):
        for dx in range(2):
            for dy in range(2):
                out[dx, dy] = fetch(info, w * 2 + dx, dy, pieces)


def load_queries(info, unit, asked, q_all):
    rows = asked[0].shape[1]
    for dy in range(2):
        block = fetch(info, unit, dy, asked)
        for g in range(GROUP):
            at = (g * 2 + dy) * rows
            q_all[at : at + rows, :] = block[:, g * HEAD : (g + 1) * HEAD]


def online_step(q, k, v, mask, state):
    top, total, mixed = state
    scores = lax.dot_general(k, q, (((1,), (1,)), ((), ())), preferred_element_type=jnp.float32)
    scores = scores * SCORE_FACTOR
    if mask is not None:
        scores = jnp.where(mask, scores, LOWEST)
    new_top = jnp.maximum(top, jnp.max(scores, axis=0, keepdims=True))
    scale = jnp.exp2(top - new_top)
    weights = jnp.exp2(scores - new_top)
    total = total * scale + jnp.sum(weights, axis=0, keepdims=True)
    mixed = mixed * scale + lax.dot_general(
        v, weights.astype(jnp.bfloat16), (((0,), (0,)), ((), ())),
        preferred_element_type=jnp.float32,
    )
    return new_top, total, mixed


def prompt_kernel(layout, slots, chunk, info, *refs):
    asked, prompt = refs[:8], refs[8:16]
    mixed_ref, top_ref, total_ref, k_all, v_all, q_all = refs[16:]
    x, core, r, y = info[0], info[1], info[2], info[3]
    rows = prompt[0].shape[0] // layout.rings
    queries = q_all.shape[0]
    for o in range(2):
        for k in range(layout.rings):
            for d in range(4):
                piece = prompt[o * 4 + d]
                group = (x ^ (d >> 1)) * 2 + (core ^ o)
                seq = lax.rem(r + layout.rings - k, layout.rings) * 2 + (y ^ (d & 1))
                at = pl.multiple_of((group * layout.rings * 2 + seq) * rows, rows)
                here = k * rows
                k_all[pl.ds(at, rows), :] = piece[here : here + rows, :HEAD]
                v_all[pl.ds(at, rows), :] = piece[here : here + rows, HEAD:]
    for n, unit in enumerate(slots):
        length, offset = unit_info(info, unit, 3), unit_info(info, unit, 4)

        @pl.when(r * (queries // GROUP) < length)
        def _():
            load_queries(info, unit, asked, q_all)

            def run(step, state, masked):
                at = pl.multiple_of(step * chunk, chunk)
                mask = None
                if masked:
                    place = lax.broadcasted_iota(jnp.int32, (chunk, queries), 0) + at
                    mask = place < offset
                return online_step(
                    q_all[...], k_all[pl.ds(at, chunk), :], v_all[pl.ds(at, chunk), :], mask, state
                )

            state = (
                jnp.full((1, queries), LOWEST, jnp.float32),
                jnp.zeros((1, queries), jnp.float32),
                jnp.zeros((HEAD, queries), jnp.float32),
            )
            whole = offset // chunk
            state = lax.fori_loop(0, whole, lambda i, s: run(i, s, False), state)
            top_ref[n], total_ref[n], mixed_ref[n] = state

            @pl.when(whole * chunk < offset)
            def _():
                state = run(whole, (top_ref[n], total_ref[n], mixed_ref[n]), True)
                top_ref[n], total_ref[n], mixed_ref[n] = state


def query_places(first, swap, rows, queries):
    column = lax.broadcasted_iota(jnp.int32, (1, queries), 1)
    for g in range(GROUP - 1, 0, -1):
        column = jnp.where(column >= g * 2 * rows, column - g * 2 * rows, column)
    second = column >= rows
    row = jnp.where(second, column - rows, column)
    upper = jnp.where(second, 1 - swap, swap)
    return first + upper * rows + row


def response_kernel(layout, w, chunk, info, *refs):
    asked, (mixed, top, total) = refs[:8], refs[8:11]
    pieces = refs[11 : 11 + layout.rings]
    outs = refs[11 + layout.rings : 15 + layout.rings]
    k_all, v_all, q_all = refs[15 + layout.rings :]
    r, y = info[2], info[3]
    rows = outs[0].shape[0]
    queries = q_all.shape[0]
    for dx in range(2):
        unit = w * 2 + dx
        length = unit_info(info, unit, 3)

        @pl.when(r * (2 * rows) >= length)
        def _():
            for dy in range(2):
                outs[dx * 2 + dy][...] = jnp.zeros((rows, WIDE), jnp.bfloat16)

        @pl.when(r * (2 * rows) < length)
        def _():
            load_queries(info, unit, asked, q_all)
            for k, piece in enumerate(pieces):
                for dy in range(2):
                    seq = lax.rem(r + layout.rings - k, layout.rings) * 2 + (y ^ dy)
                    at = pl.multiple_of(seq * rows, rows)
                    k_all[pl.ds(at, rows), :] = piece[dx, dy, :, :HEAD]
                    v_all[pl.ds(at, rows), :] = piece[dx, dy, :, HEAD:]
            place = query_places(r * (2 * rows), y, rows, queries)

            def run(step, state):
                at = pl.multiple_of(step * chunk, chunk)
                key = lax.broadcasted_iota(jnp.int32, (chunk, queries), 0) + at
                mask = key <= jnp.minimum(place, length - 1)
                return online_step(
                    q_all[...], k_all[pl.ds(at, chunk), :], v_all[pl.ds(at, chunk), :], mask, state
                )

            last = jnp.minimum((r + 1) * 2 * rows, length)
            state = (top[dx], total[dx], mixed[dx])
            _, sums, out = lax.fori_loop(0, (last + chunk - 1) // chunk, run, state)
            out = jnp.where(place < length, out / sums, 0.0).T
            for dy in range(2):
                for g in range(GROUP):
                    at = (g * 2 + dy) * rows
                    part = out[at : at + rows].astype(jnp.bfloat16)
                    outs[dx * 2 + dy][:, g * HEAD : (g + 1) * HEAD] = part


def join_kernel(*refs):
    pieces, out = refs[:-1], refs[-1]
    own = own_head()
    for w in range(out.shape[0]):
        for d in range(4):
            lane = pl.ds(pl.multiple_of((own ^ d) * WIDE, HEAD), WIDE)
            out[w, :, lane] = pieces[w * 4 + d][...]


def divisor(total, *choices):
    for choice in choices:
        if total % choice == 0:
            return choice
    return total


def struct(*shape, dtype=jnp.bfloat16):
    return jax.ShapeDtypeStruct(shape, dtype)


def after(value, *others):
    return lax.optimization_barrier((value, *others))[0]


def body(layout, q, rk, rv, pk, pv, lengths, offsets, ranks):
    cands, rows = q.shape[0], q.shape[1]
    queries = 2 * rows * GROUP
    bf16 = functools.partial(pltpu.VMEM, dtype=jnp.bfloat16)

    def both_cores(pieces):
        return pieces + [layout.permute(piece, core=1) for piece in pieces]

    info = pl.pallas_call(
        functools.partial(plan_kernel, cands),
        out_shape=struct(4 + 2 * cands * FIELDS, dtype=jnp.int32),
        in_specs=[SMEM] * 3,
        out_specs=SMEM,
        name="plan",
    )(lengths, offsets, ranks)
    prompt = layout.ring_gather(jnp.concatenate([pk, pv], axis=1))
    keys = kernel_call(
        pack_keys_kernel, [struct(cands, rows, 2 * HEAD)] * 4, (rk, rv), name="pack_keys", scalars=0
    )
    keys = layout.exchange(keys)
    asked = kernel_call(
        pack_queries_kernel,
        [struct(cands, rows, WIDE)] * 4,
        (after(q, *keys),),
        name="pack_queries",
        scalars=0,
    )
    keys = both_cores(keys)
    slots = kernel_call(
        select_keys_kernel,
        [struct(2, 2, rows, 2 * HEAD)] * cands,
        (info, *keys),
        name="select_keys",
    )
    pieces = [layout.ring_gather(slots[0])]
    prompt = kernel_call(
        functools.partial(pack_prompt_kernel, layout.rings),
        [struct(layout.rings * pk.shape[0], 2 * HEAD)] * 4,
        prompt,
        name="pack_prompt",
        scalars=0,
    )
    prompt = both_cores(layout.exchange(prompt))
    asked = both_cores(layout.exchange(asked))
    for w in range(1, cands):
        pieces.append(layout.ring_gather(after(slots[w], *prompt)))

    prompt_keys = 8 * prompt[0].shape[0]
    chunk = divisor(prompt_keys, 512, 256, 128)
    finished = []
    for w in range(cands):
        units = (w * 2, w * 2 + 1)
        state = kernel_call(
            functools.partial(prompt_kernel, layout, units, chunk),
            [
                struct(2, HEAD, queries, dtype=jnp.float32),
                struct(2, 1, queries, dtype=jnp.float32),
                struct(2, 1, queries, dtype=jnp.float32),
            ],
            (info, *asked, *prompt),
            scratch=[bf16((prompt_keys, HEAD))] * 2 + [bf16((queries, HEAD))],
            cost=(8 * queries * prompt_keys * HEAD, 4 * prompt_keys * HEAD),
            name="prompt_part",
            spare=12 << 20,
        )
        response_keys = layout.rings * 2 * rows
        outs = kernel_call(
            functools.partial(response_kernel, layout, w, divisor(response_keys, 384, 256, 128)),
            [struct(rows, WIDE)] * 4,
            (info, *asked, *state, *pieces[w]),
            scratch=[bf16((response_keys, HEAD))] * 2 + [bf16((queries, HEAD))],
            cost=(8 * queries * response_keys * HEAD, 4 * response_keys * HEAD),
            name="response_part",
            spare=12 << 20,
        )
        finished += layout.exchange(outs)
    return kernel_call(
        join_kernel, struct(*q.shape), finished, name="join_heads", scalars=0
    )


def solution(mesh):
    in_specs = (
        P("cand", "seq", None),
        P("cand", "seq", None),
        P("cand", "seq", None),
        P(("cand", "seq"), None),
        P(("cand", "seq"), None),
        P(),
        P(),
        P(),
    )
    return jax.shard_map(
        functools.partial(body, Layout(mesh)),
        mesh=mesh,
        in_specs=in_specs,
        out_specs=P("cand", "seq", None),
        check_vma=False,
    )
```

time: 131 us -> 100 us (0.76)
  the two profiles are of different devices: /device:TPU:0 before, /device:TPU:12 now
where the time goes in v2:
time: 100 us
  waiting for transfers between devices  36.8 us (37%)
  starting transfers between devices  32.5 us (32%)
  Pallas kernels  26.9 us (27%)
  local copies, waits for them, and re-layouts  4 us (4%)
    ppermute x36, waiting for transfers between devices, permute(): return lax.ppermute(array, AXES, pairs)  36.8 us
    ppermute x36, starting transfers between devices, permute(): return lax.ppermute(array, AXES, pairs)  32.5 us
    pallas_call x9, Pallas kernels, kernel_call(): pl.pallas_call(kernel, out_shape=out_shape, in_specs=[SMEM] * scalars + [...  25.6 us
    unnamed x15, local copies, waits for them, and re-layouts  3.16 us
  transfers between devices with their start and end apart: 36, of which 13 were waited for; matrix products, arithmetic and copies ran while one was open for 0% of the time, Pallas kernels for 26%

profile of v2, /device:TPU:12, one launch (start us, length us, event | category | flops | bytes accessed | tf_op | source)
XLA Modules:
  0.0 100.4 jit_solution(9677742496970054299)
XLA Ops:
  1.8 1.6 %collective-permute-start.10 = (bf16[64,1024]{1,0:T(8,128)(2,1)S(1)}, bf16[64,1024]{1,0:T(8,128)(2,1)S(1)}, u32[]{:S(2)}, u32[]{:S(2)}) collective-permute-start(bf16[64,1024]{1,0:T(8,128)(2,1)S(1)} %constant_dynamic-update-slice_fusion.refs_0_), channel_id=1, source_target_pairs={{0,2},{1,3},{2,4},{3,5},{4,6},{5,7},{6,0},{7,1},{8,10},{9,11},{10,... | collective-permute-start | bytes 393224 | tf_op jit(solution)/shard_map/ppermute | solution.py:40
  4.6 1.8 %collective-permute-start.12 = (bf16[64,1024]{1,0:T(8,128)(2,1)S(1)}, bf16[64,1024]{1,0:T(8,128)(2,1)S(1)}, u32[]{:S(2)}, u32[]{:S(2)}) collective-permute-start(bf16[64,1024]{1,0:T(8,128)(2,1)S(1)} %constant_dynamic-update-slice_fusion.refs_0_), channel_id=1, source_target_pairs={{0,6},{1,7},{2,0},{3,1},{4,2},{5,3},{6,4},{7,5},{8,14},{9,15},{10,... | collective-permute-start | bytes 393224 | tf_op jit(solution)/shard_map/ppermute | solution.py:40
  8.0 1.5 %collective-permute-start.1 = (bf16[2,96,256]{2,1,0:T(8,128)(2,1)S(1)}, bf16[2,96,256]{2,1,0:T(8,128)(2,1)S(1)}, u32[]{:S(2)}, u32[]{:S(2)}) collective-permute-start(bf16[2,96,256]{2,1,0:T(8,128)(2,1)S(1)} %get-tuple-element.37), channel_id=1, source_target_pairs={{0,16},{1,17},{2,18},{3,19},{4,20},{5,21},{6,22},{7,23},{8,24},{9,... | collective-permute-start | bytes 294920 | tf_op jit(solution)/shard_map/ppermute | solution.py:40
  9.5 3.4 %collective-permute-done.10.refs_1_ = bf16[64,1024]{1,0:T(8,128)(2,1)S(1)} collective-permute-done((bf16[64,1024]{1,0:T(8,128)(2,1)S(1)}, bf16[64,1024]{1,0:T(8,128)(2,1)S(1)}, u32[]{:S(2)}, u32[]{:S(2)}) %collective-permute-start.10) | collective-permute-done | bytes 131104 | tf_op jit(solution)/shard_map/ppermute | solution.py:40
  14.6 1.7 %collective-permute-done.12.refs_3_ = bf16[64,1024]{1,0:T(8,128)(2,1)S(1)} collective-permute-done((bf16[64,1024]{1,0:T(8,128)(2,1)S(1)}, bf16[64,1024]{1,0:T(8,128)(2,1)S(1)}, u32[]{:S(2)}, u32[]{:S(2)}) %collective-permute-start.12) | collective-permute-done | bytes 131104 | tf_op jit(solution)/shard_map/ppermute | solution.py:40
  18.4 1.5 %collective-permute-start.14 = (bf16[256,256]{1,0:T(8,128)(2,1)S(1)}, bf16[256,256]{1,0:T(8,128)(2,1)S(1)}, u32[]{:S(2)}, u32[]{:S(2)}) collective-permute-start(bf16[256,256]{1,0:T(8,128)(2,1)S(1)} %get-tuple-element.46), channel_id=1, source_target_pairs={{0,16},{1,17},{2,18},{3,19},{4,20},{5,21},{6,22},{7,23},{8,24},{9,... | collective-permute-start | bytes 393224 | tf_op jit(solution)/shard_map/ppermute | solution.py:40
  22.1 1.5 %collective-permute-start.4 = (bf16[2,96,640]{2,1,0:T(8,128)(2,1)S(1)}, bf16[2,96,640]{2,1,0:T(8,128)(2,1)S(1)}, u32[]{:S(2)}, u32[]{:S(2)}) collective-permute-start(bf16[2,96,640]{2,1,0:T(8,128)(2,1)S(1)} %get-tuple-element.42), channel_id=1, source_target_pairs={{0,16},{1,17},{2,18},{3,19},{4,20},{5,21},{6,22},{7,23},{8,24},{9,... | collective-permute-start | bytes 737288 | tf_op jit(solution)/shard_map/ppermute | solution.py:40
  24.7 3.0 %collective-permute-done.15.refs_11_ = bf16[256,256]{1,0:T(8,128)(2,1)S(1)} collective-permute-done((bf16[256,256]{1,0:T(8,128)(2,1)S(1)}, bf16[256,256]{1,0:T(8,128)(2,1)S(1)}, u32[]{:S(2)}, u32[]{:S(2)}) %collective-permute-start.15) | collective-permute-done | bytes 131104 | tf_op jit(solution)/shard_map/ppermute | solution.py:40
  28.2 3.2 %collective-permute-done.3.refs_1_ = bf16[2,96,640]{2,1,0:T(8,128)(2,1)S(1)} collective-permute-done((bf16[2,96,640]{2,1,0:T(8,128)(2,1)S(1)}, bf16[2,96,640]{2,1,0:T(8,128)(2,1)S(1)}, u32[]{:S(2)}, u32[]{:S(2)}) %collective-permute-start.3) | collective-permute-done | bytes 245792 | tf_op jit(solution)/shard_map/ppermute | solution.py:40
  32.8 5.0 %collective-permute-done.5.refs_3_ = bf16[2,96,640]{2,1,0:T(8,128)(2,1)S(1)} collective-permute-done((bf16[2,96,640]{2,1,0:T(8,128)(2,1)S(1)}, bf16[2,96,640]{2,1,0:T(8,128)(2,1)S(1)}, u32[]{:S(2)}, u32[]{:S(2)}) %collective-permute-start.5) | collective-permute-done | bytes 245792 | tf_op jit(solution)/shard_map/ppermute | solution.py:40
  41.6 2.4 %collective-permute-start.30 = (bf16[2,2,96,256]{3,2,1,0:T(8,128)(2,1)S(1)}, bf16[2,2,96,256]{3,2,1,0:T(8,128)(2,1)S(1)}, u32[]{:S(2)}, u32[]{:S(2)}) collective-permute-start(bf16[2,2,96,256]{3,2,1,0:T(8,128)(2,1)S(1)} %get-tuple-element.60.refs_11_), channel_id=1, source_target_pairs={{0,2},{1,3},{2,4},{3,5},{4,6},{5,7},{6,0},{7,1},{8,10},{9,11},{10,... | collective-permute-start | bytes 589832 | tf_op jit(solution)/shard_map/ppermute | solution.py:40
  44.0 1.5 %collective-permute-start.32 = (bf16[2,2,96,256]{3,2,1,0:T(8,128)(2,1)S(1)}, bf16[2,2,96,256]{3,2,1,0:T(8,128)(2,1)S(1)}, u32[]{:S(2)}, u32[]{:S(2)}) collective-permute-start(bf16[2,2,96,256]{3,2,1,0:T(8,128)(2,1)S(1)} %get-tuple-element.60.refs_11_), channel_id=1, source_target_pairs={{0,6},{1,7},{2,0},{3,1},{4,2},{5,3},{6,4},{7,5},{8,14},{9,15},{10,... | collective-permute-start | bytes 589832 | tf_op jit(solution)/shard_map/ppermute | solution.py:40
  46.1 4.7 %collective-permute-start.25 = (bf16[2,2,96,256]{3,2,1,0:T(8,128)(2,1)S(1)}, bf16[2,2,96,256]{3,2,1,0:T(8,128)(2,1)S(1)}, u32[]{:S(2)}, u32[]{:S(2)}) collective-permute-start(bf16[2,2,96,256]{3,2,1,0:T(8,128)(2,1)S(1)} %get-tuple-element.51.refs_11_), channel_id=1, source_target_pairs={{0,4},{1,5},{2,6},{3,7},{4,0},{5,1},{6,2},{7,3},{8,12},{9,13},{10,... | collective-permute-start | bytes 589832 | tf_op jit(solution)/shard_map/ppermute | solution.py:40
  50.7 7.2 %prompt_part.3 = (f32[2,128,960]{2,1,0:T(8,128)S(1)}, f32[2,1,960]{2,1,0:T(1,128)S(1)}, f32[2,1,960]{2,1,0:T(1,128)S(1)}) custom-call(s32[24]{0:T(128)S(1)} %copy-done.4, bf16[2,96,640]{2,1,0:T(8,128)(2,1)S(1)} %get-tuple-element.40.refs_0_, bf16[2,96,640]{2,1,0:T(8,128)(2,1)S(1)} %collective-permute-done.3.refs_1_, ...), custom_call_target="tpu_custom_call" | custom-call | flops 2013265920 | bytes 1048576 | tf_op jit(solution)/shard_map/prompt_part/pallas_call | solution.py:53
  58.0 12.2 %collective-permute-done.31.refs_13_ = bf16[2,2,96,256]{3,2,1,0:T(8,128)(2,1)S(1)} collective-permute-done((bf16[2,2,96,256]{3,2,1,0:T(8,128)(2,1)S(1)}, bf16[2,2,96,256]{3,2,1,0:T(8,128)(2,1)S(1)}, u32[]{:S(2)}, u32[]{:S(2)}) %collective-permute-start.31) | collective-permute-done | bytes 196640 | tf_op jit(solution)/shard_map/ppermute | solution.py:40
  70.3 3.5 %response_part.3 = (bf16[96,640]{1,0:T(8,128)(2,1)S(1)}, bf16[96,640]{1,0:T(8,128)(2,1)S(1)}, bf16[96,640]{1,0:T(8,128)(2,1)S(1)}, bf16[96,640]{1,0:T(8,128)(2,1)S(1)}) custom-call(s32[24]{0:T(128)S(1)} %copy-done.4, bf16[2,96,640]{2,1,0:T(8,128)(2,1)S(1)} %get-tuple-element.40.refs_0_, bf16[2,96,640]{2,1,0:T(8,128)(2,1)S(1)} %collective-permute-done.3.refs_1_, ...), custom_call_target="tpu_custom_call" | custom-call | flops 754974720 | bytes 393216 | tf_op jit(solution)/shard_map/response_part/pallas_call | solution.py:53
  73.7 1.7 %collective-permute-start.33 = (bf16[96,640]{1,0:T(8,128)(2,1)S(1)}, bf16[96,640]{1,0:T(8,128)(2,1)S(1)}, u32[]{:S(2)}, u32[]{:S(2)}) collective-permute-start(bf16[96,640]{1,0:T(8,128)(2,1)S(1)} %get-tuple-element.62), channel_id=1, source_target_pairs={{0,1},{1,0},{2,3},{3,2},{4,5},{5,4},{6,7},{7,6},{8,9},{9,8},{10,11... | collective-permute-start | bytes 368648 | tf_op jit(solution)/shard_map/ppermute | solution.py:40
  75.4 1.5 %collective-permute-start.34 = (bf16[96,640]{1,0:T(8,128)(2,1)S(1)}, bf16[96,640]{1,0:T(8,128)(2,1)S(1)}, u32[]{:S(2)}, u32[]{:S(2)}) collective-permute-start(bf16[96,640]{1,0:T(8,128)(2,1)S(1)} %get-tuple-element.63), channel_id=1, source_target_pairs={{0,16},{1,17},{2,18},{3,19},{4,20},{5,21},{6,22},{7,23},{8,24},{9,... | collective-permute-start | bytes 368648 | tf_op jit(solution)/shard_map/ppermute | solution.py:40
  76.9 9.5 %prompt_part.2 = (f32[2,128,960]{2,1,0:T(8,128)S(1)}, f32[2,1,960]{2,1,0:T(1,128)S(1)}, f32[2,1,960]{2,1,0:T(1,128)S(1)}) custom-call(s32[24]{0:T(128)S(1)} %copy-done.4, bf16[2,96,640]{2,1,0:T(8,128)(2,1)S(1)} %get-tuple-element.40.refs_0_, bf16[2,96,640]{2,1,0:T(8,128)(2,1)S(1)} %collective-permute-done.3.refs_1_, ...), custom_call_target="tpu_custom_call" | custom-call | flops 2013265920 | bytes 1048576 | tf_op jit(solution)/shard_map/prompt_part/pallas_call | solution.py:53
  86.9 3.5 %response_part.2 = (bf16[96,640]{1,0:T(8,128)(2,1)S(1)}, bf16[96,640]{1,0:T(8,128)(2,1)S(1)}, bf16[96,640]{1,0:T(8,128)(2,1)S(1)}, bf16[96,640]{1,0:T(8,128)(2,1)S(1)}) custom-call(s32[24]{0:T(128)S(1)} %copy-done.4, bf16[2,96,640]{2,1,0:T(8,128)(2,1)S(1)} %get-tuple-element.40.refs_0_, bf16[2,96,640]{2,1,0:T(8,128)(2,1)S(1)} %collective-permute-done.3.refs_1_, ...), custom_call_target="tpu_custom_call" | custom-call | flops 754974720 | bytes 393216 | tf_op jit(solution)/shard_map/response_part/pallas_call | solution.py:53
  90.4 1.7 %collective-permute-start.27 = (bf16[96,640]{1,0:T(8,128)(2,1)S(1)}, bf16[96,640]{1,0:T(8,128)(2,1)S(1)}, u32[]{:S(2)}, u32[]{:S(2)}) collective-permute-start(bf16[96,640]{1,0:T(8,128)(2,1)S(1)} %get-tuple-element.53), channel_id=1, source_target_pairs={{0,1},{1,0},{2,3},{3,2},{4,5},{5,4},{6,7},{7,6},{8,9},{9,8},{10,11... | collective-permute-start | bytes 368648 | tf_op jit(solution)/shard_map/ppermute | solution.py:40
  92.0 1.5 %collective-permute-start.28 = (bf16[96,640]{1,0:T(8,128)(2,1)S(1)}, bf16[96,640]{1,0:T(8,128)(2,1)S(1)}, u32[]{:S(2)}, u32[]{:S(2)}) collective-permute-start(bf16[96,640]{1,0:T(8,128)(2,1)S(1)} %get-tuple-element.54), channel_id=1, source_target_pairs={{0,16},{1,17},{2,18},{3,19},{4,20},{5,21},{6,22},{7,23},{8,24},{9,... | collective-permute-start | bytes 368648 | tf_op jit(solution)/shard_map/ppermute | solution.py:40
  93.9 2.6 %collective-permute-done.27.refs_1_ = bf16[96,640]{1,0:T(8,128)(2,1)S(1)} collective-permute-done((bf16[96,640]{1,0:T(8,128)(2,1)S(1)}, bf16[96,640]{1,0:T(8,128)(2,1)S(1)}, u32[]{:S(2)}, u32[]{:S(2)}) %collective-permute-start.27) | collective-permute-done | bytes 122912 | tf_op jit(solution)/shard_map/ppermute | solution.py:40
  96.9 2.4 %collective-permute-done.29.refs_3_ = bf16[96,640]{1,0:T(8,128)(2,1)S(1)} collective-permute-done((bf16[96,640]{1,0:T(8,128)(2,1)S(1)}, bf16[96,640]{1,0:T(8,128)(2,1)S(1)}, u32[]{:S(2)}, u32[]{:S(2)}) %collective-permute-start.29) | collective-permute-done | bytes 122912 | tf_op jit(solution)/shard_map/ppermute | solution.py:40
  (74 shorter events, 20.2 us)
Async XLA Ops:
  1.8 11.1 %collective-permute-start.10 = (bf16[64,1024]{1,0:T(8,128)(2,1)S(1)}, bf16[64,1024]{1,0:T(8,128)(2,1)S(1)}, u32[]{:S(2)}, u32[]{:S(2)}) collective-permute-start(bf16[64,1024]{1,0:T(8,128)(2,1)S(1)} %constant_dynamic-update-slice_fusion.refs_0_), channel_id=1, source_target_pairs={{0,2},{1,3},{2,4},{3,5},{4,6},{5,7},{6,0},{7,1},{8,10},{9,11},{10,... | collective-permute-start | bytes 393224 | tf_op jit(solution)/shard_map/ppermute | solution.py:40
  3.4 11.2 %collective-permute-start.11 = (bf16[64,1024]{1,0:T(8,128)(2,1)S(1)}, bf16[64,1024]{1,0:T(8,128)(2,1)S(1)}, u32[]{:S(2)}, u32[]{:S(2)}) collective-permute-start(bf16[64,1024]{1,0:T(8,128)(2,1)S(1)} %constant_dynamic-update-slice_fusion.refs_0_), channel_id=1, source_target_pairs={{0,4},{1,5},{2,6},{3,7},{4,0},{5,1},{6,2},{7,3},{8,12},{9,13},{10,... | collective-permute-start | bytes 393224 | tf_op jit(solution)/shard_map/ppermute | solution.py:40
  4.6 11.7 %collective-permute-start.12 = (bf16[64,1024]{1,0:T(8,128)(2,1)S(1)}, bf16[64,1024]{1,0:T(8,128)(2,1)S(1)}, u32[]{:S(2)}, u32[]{:S(2)}) collective-permute-start(bf16[64,1024]{1,0:T(8,128)(2,1)S(1)} %constant_dynamic-update-slice_fusion.refs_0_), channel_id=1, source_target_pairs={{0,6},{1,7},{2,0},{3,1},{4,2},{5,3},{6,4},{7,5},{8,14},{9,15},{10,... | collective-permute-start | bytes 393224 | tf_op jit(solution)/shard_map/ppermute | solution.py:40
  7.4 9.6 %collective-permute-start = (bf16[2,96,256]{2,1,0:T(8,128)(2,1)S(1)}, bf16[2,96,256]{2,1,0:T(8,128)(2,1)S(1)}, u32[]{:S(2)}, u32[]{:S(2)}) collective-permute-start(bf16[2,96,256]{2,1,0:T(8,128)(2,1)S(1)} %get-tuple-element.36), channel_id=1, source_target_pairs={{0,1},{1,0},{2,3},{3,2},{4,5},{5,4},{6,7},{7,6},{8,9},{9,8},{10,11... | collective-permute-start | bytes 294920 | tf_op jit(solution)/shard_map/ppermute | solution.py:40
  8.0 9.0 %collective-permute-start.1 = (bf16[2,96,256]{2,1,0:T(8,128)(2,1)S(1)}, bf16[2,96,256]{2,1,0:T(8,128)(2,1)S(1)}, u32[]{:S(2)}, u32[]{:S(2)}) collective-permute-start(bf16[2,96,256]{2,1,0:T(8,128)(2,1)S(1)} %get-tuple-element.37), channel_id=1, source_target_pairs={{0,16},{1,17},{2,18},{3,19},{4,20},{5,21},{6,22},{7,23},{8,24},{9,... | collective-permute-start | bytes 294920 | tf_op jit(solution)/shard_map/ppermute | solution.py:40
  19.9 7.8 %collective-permute-start.15 = (bf16[256,256]{1,0:T(8,128)(2,1)S(1)}, bf16[256,256]{1,0:T(8,128)(2,1)S(1)}, u32[]{:S(2)}, u32[]{:S(2)}) collective-permute-start(bf16[256,256]{1,0:T(8,128)(2,1)S(1)} %get-tuple-element.47), channel_id=1, source_target_pairs={{0,17},{1,16},{2,19},{3,18},{4,21},{5,20},{6,23},{7,22},{8,25},{9,... | collective-permute-start | bytes 393224 | tf_op jit(solution)/shard_map/ppermute | solution.py:40
  20.9 10.6 %collective-permute-start.3 = (bf16[2,96,640]{2,1,0:T(8,128)(2,1)S(1)}, bf16[2,96,640]{2,1,0:T(8,128)(2,1)S(1)}, u32[]{:S(2)}, u32[]{:S(2)}) collective-permute-start(bf16[2,96,640]{2,1,0:T(8,128)(2,1)S(1)} %get-tuple-element.41), channel_id=1, source_target_pairs={{0,1},{1,0},{2,3},{3,2},{4,5},{5,4},{6,7},{7,6},{8,9},{9,8},{10,11... | collective-permute-start | bytes 737288 | tf_op jit(solution)/shard_map/ppermute | solution.py:40
  22.1 10.8 %collective-permute-start.4 = (bf16[2,96,640]{2,1,0:T(8,128)(2,1)S(1)}, bf16[2,96,640]{2,1,0:T(8,128)(2,1)S(1)}, u32[]{:S(2)}, u32[]{:S(2)}) collective-permute-start(bf16[2,96,640]{2,1,0:T(8,128)(2,1)S(1)} %get-tuple-element.42), channel_id=1, source_target_pairs={{0,16},{1,17},{2,18},{3,19},{4,20},{5,21},{6,22},{7,23},{8,24},{9,... | collective-permute-start | bytes 737288 | tf_op jit(solution)/shard_map/ppermute | solution.py:40
  23.6 14.2 %collective-permute-start.5 = (bf16[2,96,640]{2,1,0:T(8,128)(2,1)S(1)}, bf16[2,96,640]{2,1,0:T(8,128)(2,1)S(1)}, u32[]{:S(2)}, u32[]{:S(2)}) collective-permute-start(bf16[2,96,640]{2,1,0:T(8,128)(2,1)S(1)} %get-tuple-element.43), channel_id=1, source_target_pairs={{0,17},{1,16},{2,19},{3,18},{4,21},{5,20},{6,23},{7,22},{8,25},{9,... | collective-permute-start | bytes 737288 | tf_op jit(solution)/shard_map/ppermute | solution.py:40
  27.7 10.1 %collective-permute-start.17 = (bf16[256,256]{1,0:T(8,128)(2,1)S(1)}, bf16[256,256]{1,0:T(8,128)(2,1)S(1)}, u32[]{:S(2)}, u32[]{:S(2)}) collective-permute-start(bf16[256,256]{1,0:T(8,128)(2,1)S(1)} %collective-permute-done.13.refs_9_), channel_id=1, source_target_pairs={{0,8},{1,9},{2,10},{3,11},{4,12},{5,13},{6,14},{7,15},{8,0},{9,1},... | collective-permute-start | bytes 393224 | tf_op jit(solution)/shard_map/ppermute | solution.py:40
  27.7 10.6 %collective-permute-start.18 = (bf16[256,256]{1,0:T(8,128)(2,1)S(1)}, bf16[256,256]{1,0:T(8,128)(2,1)S(1)}, u32[]{:S(2)}, u32[]{:S(2)}) collective-permute-start(bf16[256,256]{1,0:T(8,128)(2,1)S(1)} %collective-permute-done.14.refs_10_), channel_id=1, source_target_pairs={{0,8},{1,9},{2,10},{3,11},{4,12},{5,13},{6,14},{7,15},{8,0},{9,1},... | collective-permute-start | bytes 393224 | tf_op jit(solution)/shard_map/ppermute | solution.py:40
  31.5 12.5 %collective-permute-start.6 = (bf16[2,96,640]{2,1,0:T(8,128)(2,1)S(1)}, bf16[2,96,640]{2,1,0:T(8,128)(2,1)S(1)}, u32[]{:S(2)}, u32[]{:S(2)}) collective-permute-start(bf16[2,96,640]{2,1,0:T(8,128)(2,1)S(1)} %get-tuple-element.40.refs_0_), channel_id=1, source_target_pairs={{0,8},{1,9},{2,10},{3,11},{4,12},{5,13},{6,14},{7,15},{8,0},{9,1},... | collective-permute-start | bytes 737288 | tf_op jit(solution)/shard_map/ppermute | solution.py:40
  32.8 11.2 %collective-permute-start.7 = (bf16[2,96,640]{2,1,0:T(8,128)(2,1)S(1)}, bf16[2,96,640]{2,1,0:T(8,128)(2,1)S(1)}, u32[]{:S(2)}, u32[]{:S(2)}) collective-permute-start(bf16[2,96,640]{2,1,0:T(8,128)(2,1)S(1)} %collective-permute-done.3.refs_1_), channel_id=1, source_target_pairs={{0,8},{1,9},{2,10},{3,11},{4,12},{5,13},{6,14},{7,15},{8,0},{9,1},... | collective-permute-start | bytes 737288 | tf_op jit(solution)/shard_map/ppermute | solution.py:40
  37.8 7.7 %collective-permute-start.8 = (bf16[2,96,640]{2,1,0:T(8,128)(2,1)S(1)}, bf16[2,96,640]{2,1,0:T(8,128)(2,1)S(1)}, u32[]{:S(2)}, u32[]{:S(2)}) collective-permute-start(bf16[2,96,640]{2,1,0:T(8,128)(2,1)S(1)} %collective-permute-done.4.refs_2_), channel_id=1, source_target_pairs={{0,8},{1,9},{2,10},{3,11},{4,12},{5,13},{6,14},{7,15},{8,0},{9,1},... | collective-permute-start | bytes 737288 | tf_op jit(solution)/shard_map/ppermute | solution.py:40
  37.8 8.3 %collective-permute-start.9 = (bf16[2,96,640]{2,1,0:T(8,128)(2,1)S(1)}, bf16[2,96,640]{2,1,0:T(8,128)(2,1)S(1)}, u32[]{:S(2)}, u32[]{:S(2)}) collective-permute-start(bf16[2,96,640]{2,1,0:T(8,128)(2,1)S(1)} %collective-permute-done.5.refs_3_), channel_id=1, source_target_pairs={{0,8},{1,9},{2,10},{3,11},{4,12},{5,13},{6,14},{7,15},{8,0},{9,1},... | collective-permute-start | bytes 737288 | tf_op jit(solution)/shard_map/ppermute | solution.py:40
  41.6 16.3 %collective-permute-start.30 = (bf16[2,2,96,256]{3,2,1,0:T(8,128)(2,1)S(1)}, bf16[2,2,96,256]{3,2,1,0:T(8,128)(2,1)S(1)}, u32[]{:S(2)}, u32[]{:S(2)}) collective-permute-start(bf16[2,2,96,256]{3,2,1,0:T(8,128)(2,1)S(1)} %get-tuple-element.60.refs_11_), channel_id=1, source_target_pairs={{0,2},{1,3},{2,4},{3,5},{4,6},{5,7},{6,0},{7,1},{8,10},{9,11},{10,... | collective-permute-start | bytes 589832 | tf_op jit(solution)/shard_map/ppermute | solution.py:40
  44.0 26.3 %collective-permute-start.31 = (bf16[2,2,96,256]{3,2,1,0:T(8,128)(2,1)S(1)}, bf16[2,2,96,256]{3,2,1,0:T(8,128)(2,1)S(1)}, u32[]{:S(2)}, u32[]{:S(2)}) collective-permute-start(bf16[2,2,96,256]{3,2,1,0:T(8,128)(2,1)S(1)} %get-tuple-element.60.refs_11_), channel_id=1, source_target_pairs={{0,4},{1,5},{2,6},{3,7},{4,0},{5,1},{6,2},{7,3},{8,12},{9,13},{10,... | collective-permute-start | bytes 589832 | tf_op jit(solution)/shard_map/ppermute | solution.py:40
  44.0 26.3 %collective-permute-start.32 = (bf16[2,2,96,256]{3,2,1,0:T(8,128)(2,1)S(1)}, bf16[2,2,96,256]{3,2,1,0:T(8,128)(2,1)S(1)}, u32[]{:S(2)}, u32[]{:S(2)}) collective-permute-start(bf16[2,2,96,256]{3,2,1,0:T(8,128)(2,1)S(1)} %get-tuple-element.60.refs_11_), channel_id=1, source_target_pairs={{0,6},{1,7},{2,0},{3,1},{4,2},{5,3},{6,4},{7,5},{8,14},{9,15},{10,... | collective-permute-start | bytes 589832 | tf_op jit(solution)/shard_map/ppermute | solution.py:40
  45.5 40.9 %collective-permute-start.24 = (bf16[2,2,96,256]{3,2,1,0:T(8,128)(2,1)S(1)}, bf16[2,2,96,256]{3,2,1,0:T(8,128)(2,1)S(1)}, u32[]{:S(2)}, u32[]{:S(2)}) collective-permute-start(bf16[2,2,96,256]{3,2,1,0:T(8,128)(2,1)S(1)} %get-tuple-element.51.refs_11_), channel_id=1, source_target_pairs={{0,2},{1,3},{2,4},{3,5},{4,6},{5,7},{6,0},{7,1},{8,10},{9,11},{10,... | collective-permute-start | bytes 589832 | tf_op jit(solution)/shard_map/ppermute | solution.py:40
  46.1 40.8 %collective-permute-start.25 = (bf16[2,2,96,256]{3,2,1,0:T(8,128)(2,1)S(1)}, bf16[2,2,96,256]{3,2,1,0:T(8,128)(2,1)S(1)}, u32[]{:S(2)}, u32[]{:S(2)}) collective-permute-start(bf16[2,2,96,256]{3,2,1,0:T(8,128)(2,1)S(1)} %get-tuple-element.51.refs_11_), channel_id=1, source_target_pairs={{0,4},{1,5},{2,6},{3,7},{4,0},{5,1},{6,2},{7,3},{8,12},{9,13},{10,... | collective-permute-start | bytes 589832 | tf_op jit(solution)/shard_map/ppermute | solution.py:40
  57.9 29.0 %collective-permute-start.26 = (bf16[2,2,96,256]{3,2,1,0:T(8,128)(2,1)S(1)}, bf16[2,2,96,256]{3,2,1,0:T(8,128)(2,1)S(1)}, u32[]{:S(2)}, u32[]{:S(2)}) collective-permute-start(bf16[2,2,96,256]{3,2,1,0:T(8,128)(2,1)S(1)} %get-tuple-element.51.refs_11_), channel_id=1, source_target_pairs={{0,6},{1,7},{2,0},{3,1},{4,2},{5,3},{6,4},{7,5},{8,14},{9,15},{10,... | collective-permute-start | bytes 589832 | tf_op jit(solution)/shard_map/ppermute | solution.py:40
  73.7 19.8 %collective-permute-start.33 = (bf16[96,640]{1,0:T(8,128)(2,1)S(1)}, bf16[96,640]{1,0:T(8,128)(2,1)S(1)}, u32[]{:S(2)}, u32[]{:S(2)}) collective-permute-start(bf16[96,640]{1,0:T(8,128)(2,1)S(1)} %get-tuple-element.62), channel_id=1, source_target_pairs={{0,1},{1,0},{2,3},{3,2},{4,5},{5,4},{6,7},{7,6},{8,9},{9,8},{10,11... | collective-permute-start | bytes 368648 | tf_op jit(solution)/shard_map/ppermute | solution.py:40
  75.4 18.5 %collective-permute-start.34 = (bf16[96,640]{1,0:T(8,128)(2,1)S(1)}, bf16[96,640]{1,0:T(8,128)(2,1)S(1)}, u32[]{:S(2)}, u32[]{:S(2)}) collective-permute-start(bf16[96,640]{1,0:T(8,128)(2,1)S(1)} %get-tuple-element.63), channel_id=1, source_target_pairs={{0,16},{1,17},{2,18},{3,19},{4,20},{5,21},{6,22},{7,23},{8,24},{9,... | collective-permute-start | bytes 368648 | tf_op jit(solution)/shard_map/ppermute | solution.py:40
  86.4 7.5 %collective-permute-start.35 = (bf16[96,640]{1,0:T(8,128)(2,1)S(1)}, bf16[96,640]{1,0:T(8,128)(2,1)S(1)}, u32[]{:S(2)}, u32[]{:S(2)}) collective-permute-start(bf16[96,640]{1,0:T(8,128)(2,1)S(1)} %get-tuple-element.64), channel_id=1, source_target_pairs={{0,17},{1,16},{2,19},{3,18},{4,21},{5,20},{6,23},{7,22},{8,25},{9,... | collective-permute-start | bytes 368648 | tf_op jit(solution)/shard_map/ppermute | solution.py:40
  (19 other events, 104.0 us)

commit v3 on v2

--- a/solution.py
+++ b/solution.py
@@ -42,8 +42,14 @@
     def exchange(self, pieces):
         return [pieces[0]] + [self.permute(pieces[d], d=d) for d in range(1, 4)]
 
+    def spread(self, block):
+        return [block] + [self.permute(block, ring=k) for k in range(1, self.rings)]
+
     def ring_gather(self, block):
-        return [block] + [self.permute(block, ring=k) for k in range(1, self.rings)]
+        pieces = [block]
+        for _ in range(self.rings - 1):
+            pieces.append(self.permute(pieces[-1], ring=1))
+        return pieces
 
 
 def kernel_call(kernel, out_shape, operands, scratch=(), cost=(0, 0), name=None, scalars=1, spare=2 << 20):
@@ -92,57 +98,61 @@
 
 def pack_keys_kernel(rk, rv, *outs):
     own = own_head()
+    cands, rows = rk.shape[0], rk.shape[1]
     for d, out in enumerate(outs):
         lane = pl.ds(pl.multiple_of((own ^ d) * HEAD, HEAD), HEAD)
-        out[:, :, :HEAD] = rk[:, :, lane]
-        out[:, :, HEAD:] = rv[:, :, lane]
-
-
-def pack_prompt_kernel(rings, *refs):
+        for w in range(cands):
+            out[w * rows : (w + 1) * rows, :HEAD] = rk[w, :, lane]
+            out[w * rows : (w + 1) * rows, HEAD:] = rv[w, :, lane]
+
+
+def pack_kernel(rings, q, *refs):
     pieces, outs = refs[:rings], refs[rings:]
     own = own_head()
-    rows, width = pieces[0].shape
+    cands, rows = q.shape[0], q.shape[1]
+    prompt_rows, width = pieces[0].shape
     for d, out in enumerate(outs):
-        lane = pl.multiple_of((own ^ d) * HEAD, HEAD)
-        for k, piece in enumerate(pieces):
-            out[k * rows : (k + 1) * rows, :HEAD] = piece[:, pl.ds(lane, HEAD)]
-            out[k * rows : (k + 1) * rows, HEAD:] = piece[:, pl.ds(lane + width // 2, HEAD)]
-
-
-def pack_queries_kernel(q, *outs):
-    own = own_head()
-    for d, out in enumerate(outs):
-        lane = pl.ds(pl.multiple_of((own ^ d) * WIDE, HEAD), WIDE)
-        for w in range(q.shape[0]):
-            out[w] = q[w, :, lane]
+        for w in range(cands):
+            for g in range(GROUP):
+                lane = pl.multiple_of((own ^ d) * WIDE + g * HEAD, HEAD)
+                at = (w * GROUP + g) * rows
+                out[at : at + rows, :] = q[w, :, pl.ds(lane, HEAD)]
+        for half in range(2):
+            lane = pl.multiple_of((own ^ d) * HEAD + half * (width // 2), HEAD)
+            for k, piece in enumerate(pieces):
+                at = cands * GROUP * rows + (half * rings + k) * prompt_rows
+                out[at : at + prompt_rows, :] = piece[:, pl.ds(lane, HEAD)]
 
 
 def unit_info(info, unit, field):
     return info[4 + unit * FIELDS + field]
 
 
-def fetch(info, unit, dy, pieces):
-    away, home, slot = (unit_info(info, unit, n) for n in range(3))
-    near = jnp.where(home == 1, pieces[2 + dy][slot], pieces[dy][slot])
-    far = jnp.where(home == 1, pieces[6 + dy][slot], pieces[4 + dy][slot])
+def fetch(info, unit, dy, pieces, row, rows):
+    away, home = unit_info(info, unit, 0), unit_info(info, unit, 1)
+    at = pl.ds(pl.multiple_of(row, rows), rows)
+    near = jnp.where(home == 1, pieces[2 + dy][at, :], pieces[dy][at, :])
+    far = jnp.where(home == 1, pieces[6 + dy][at, :], pieces[4 + dy][at, :])
     return jnp.where(away == 1, far, near)
 
 
 def select_keys_kernel(info, *refs):
     pieces, outs = refs[:8], refs[8:]
+    rows = outs[0].shape[2]
     for w, out in enumerate(outs):
         for dx in range(2):
+            unit = w * 2 + dx
             for dy in range(2):
-                out[dx, dy] = fetch(info, w * 2 + dx, dy, pieces)
-
-
-def load_queries(info, unit, asked, q_all):
-    rows = asked[0].shape[1]
+                out[dx, dy] = fetch(info, unit, dy, pieces, unit_info(info, unit, 2) * rows, rows)
+
+
+def load_queries(info, unit, packed, q_all):
+    rows = q_all.shape[0] // (2 * GROUP)
     for dy in range(2):
-        block = fetch(info, unit, dy, asked)
         for g in range(GROUP):
+            row = (unit_info(info, unit, 2) * GROUP + g) * rows
             at = (g * 2 + dy) * rows
-            q_all[at : at + rows, :] = block[:, g * HEAD : (g + 1) * HEAD]
+            q_all[at : at + rows, :] = fetch(info, unit, dy, packed, row, rows)
 
 
 def online_step(q, k, v, mask, state):
@@ -163,27 +173,29 @@
 
 
 def prompt_kernel(layout, slots, chunk, info, *refs):
-    asked, prompt = refs[:8], refs[8:16]
-    mixed_ref, top_ref, total_ref, k_all, v_all, q_all = refs[16:]
+    packed = refs[:8]
+    mixed_ref, top_ref, total_ref, k_all, v_all, q_all = refs[8:]
     x, core, r, y = info[0], info[1], info[2], info[3]
-    rows = prompt[0].shape[0] // layout.rings
+    rows = k_all.shape[0] // (layout.rings * 8)
     queries = q_all.shape[0]
+    first = packed[0].shape[0] - 2 * layout.rings * rows
     for o in range(2):
         for k in range(layout.rings):
             for d in range(4):
-                piece = prompt[o * 4 + d]
+                piece = packed[o * 4 + d]
                 group = (x ^ (d >> 1)) * 2 + (core ^ o)
                 seq = lax.rem(r + layout.rings - k, layout.rings) * 2 + (y ^ (d & 1))
                 at = pl.multiple_of((group * layout.rings * 2 + seq) * rows, rows)
-                here = k * rows
-                k_all[pl.ds(at, rows), :] = piece[here : here + rows, :HEAD]
-                v_all[pl.ds(at, rows), :] = piece[here : here + rows, HEAD:]
+                here = first + k * rows
+                k_all[pl.ds(at, rows), :] = piece[here : here + rows, :]
+                here += layout.rings * rows
+                v_all[pl.ds(at, rows), :] = piece[here : here + rows, :]
     for n, unit in enumerate(slots):
         length, offset = unit_info(info, unit, 3), unit_info(info, unit, 4)
 
         @pl.when(r * (queries // GROUP) < length)
         def _():
-            load_queries(info, unit, asked, q_all)
+            load_queries(info, unit, packed, q_all)
 
             def run(step, state, masked):
                 at = pl.multiple_of(step * chunk, chunk)
@@ -220,51 +232,50 @@
     return first + upper * rows + row
 
 
-def response_kernel(layout, w, chunk, info, *refs):
-    asked, (mixed, top, total) = refs[:8], refs[8:11]
+def response_kernel(layout, w, dx, chunk, info, *refs):
+    packed, (mixed, top, total) = refs[:8], refs[8:11]
     pieces = refs[11 : 11 + layout.rings]
-    outs = refs[11 + layout.rings : 15 + layout.rings]
-    k_all, v_all, q_all = refs[15 + layout.rings :]
+    outs = refs[11 + layout.rings : 13 + layout.rings]
+    k_all, v_all, q_all = refs[13 + layout.rings :]
     r, y = info[2], info[3]
     rows = outs[0].shape[0]
     queries = q_all.shape[0]
-    for dx in range(2):
-        unit = w * 2 + dx
-        length = unit_info(info, unit, 3)
-
-        @pl.when(r * (2 * rows) >= length)
-        def _():
+    unit = w * 2 + dx
+    length = unit_info(info, unit, 3)
+
+    @pl.when(r * (2 * rows) >= length)
+    def _():
+        for out in outs:
+            out[...] = jnp.zeros(out.shape, out.dtype)
+
+    @pl.when(r * (2 * rows) < length)
+    def _():
+        load_queries(info, unit, packed, q_all)
+        for k, piece in enumerate(pieces):
             for dy in range(2):
-                outs[dx * 2 + dy][...] = jnp.zeros((rows, WIDE), jnp.bfloat16)
-
-        @pl.when(r * (2 * rows) < length)
-        def _():
-            load_queries(info, unit, asked, q_all)
-            for k, piece in enumerate(pieces):
-                for dy in range(2):
-                    seq = lax.rem(r + layout.rings - k, layout.rings) * 2 + (y ^ dy)
-                    at = pl.multiple_of(seq * rows, rows)
-                    k_all[pl.ds(at, rows), :] = piece[dx, dy, :, :HEAD]
-                    v_all[pl.ds(at, rows), :] = piece[dx, dy, :, HEAD:]
-            place = query_places(r * (2 * rows), y, rows, queries)
-
-            def run(step, state):
-                at = pl.multiple_of(step * chunk, chunk)
-                key = lax.broadcasted_iota(jnp.int32, (chunk, queries), 0) + at
-                mask = key <= jnp.minimum(place, length - 1)
-                return online_step(
-                    q_all[...], k_all[pl.ds(at, chunk), :], v_all[pl.ds(at, chunk), :], mask, state
-                )
-
-            last = jnp.minimum((r + 1) * 2 * rows, length)
-            state = (top[dx], total[dx], mixed[dx])
-            _, sums, out = lax.fori_loop(0, (last + chunk - 1) // chunk, run, state)
-            out = jnp.where(place < length, out / sums, 0.0).T
-            for dy in range(2):
-                for g in range(GROUP):
-                    at = (g * 2 + dy) * rows
-                    part = out[at : at + rows].astype(jnp.bfloat16)
-                    outs[dx * 2 + dy][:, g * HEAD : (g + 1) * HEAD] = part
+                seq = lax.rem(r + layout.rings - k, layout.rings) * 2 + (y ^ dy)
+                at = pl.multiple_of(seq * rows, rows)
+                k_all[pl.ds(at, rows), :] = piece[dx, dy, :, :HEAD]
+                v_all[pl.ds(at, rows), :] = piece[dx, dy, :, HEAD:]
+        place = query_places(r * (2 * rows), y, rows, queries)
+
+        def run(step, state):
+            at = pl.multiple_of(step * chunk, chunk)
+            key = lax.broadcasted_iota(jnp.int32, (chunk, queries), 0) + at
+            mask = key <= jnp.minimum(place, length - 1)
+            return online_step(
+                q_all[...], k_all[pl.ds(at, chunk), :], v_all[pl.ds(at, chunk), :], mask, state
+            )
+
+        last = jnp.minimum((r + 1) * 2 * rows, length)
+        state = (top[dx], total[dx], mixed[dx])
+        _, sums, result = lax.fori_loop(0, (last + chunk - 1) // chunk, run, state)
+        result = jnp.where(place < length, result / sums, 0.0).T
+        for dy, out in enumerate(outs):
+            for g in range(GROUP):
+                at = (g * 2 + dy) * rows
+                part = result[at : at + rows].astype(jnp.bfloat16)
+                out[:, g * HEAD : (g + 1) * HEAD] = part
 
 
 def join_kernel(*refs):
@@ -306,19 +317,11 @@
         out_specs=SMEM,
         name="plan",
     )(lengths, offsets, ranks)
-    prompt = layout.ring_gather(jnp.concatenate([pk, pv], axis=1))
+    prompt = layout.spread(jnp.concatenate([pk, pv], axis=1))
     keys = kernel_call(
-        pack_keys_kernel, [struct(cands, rows, 2 * HEAD)] * 4, (rk, rv), name="pack_keys", scalars=0
-    )
-    keys = layout.exchange(keys)
-    asked = kernel_call(
-        pack_queries_kernel,
-        [struct(cands, rows, WIDE)] * 4,
-        (after(q, *keys),),
-        name="pack_queries",
-        scalars=0,
-    )
-    keys = both_cores(keys)
+        pack_keys_kernel, [struct(cands * rows, 2 * HEAD)] * 4, (rk, rv), name="pack_keys", scalars=0
+    )
+    keys = both_cores(layout.exchange(keys))
     slots = kernel_call(
         select_keys_kernel,
         [struct(2, 2, rows, 2 * HEAD)] * cands,
@@ -326,50 +329,51 @@
         name="select_keys",
     )
     pieces = [layout.ring_gather(slots[0])]
-    prompt = kernel_call(
-        functools.partial(pack_prompt_kernel, layout.rings),
-        [struct(layout.rings * pk.shape[0], 2 * HEAD)] * 4,
-        prompt,
-        name="pack_prompt",
+    prompt_rows = layout.rings * pk.shape[0]
+    packed = kernel_call(
+        functools.partial(pack_kernel, layout.rings),
+        [struct(cands * GROUP * rows + 2 * prompt_rows, HEAD)] * 4,
+        (after(q, slots[0]), *prompt),
+        name="pack_queries_prompt",
         scalars=0,
     )
-    prompt = both_cores(layout.exchange(prompt))
-    asked = both_cores(layout.exchange(asked))
+    packed = both_cores(layout.exchange(packed))
     for w in range(1, cands):
-        pieces.append(layout.ring_gather(after(slots[w], *prompt)))
-
-    prompt_keys = 8 * prompt[0].shape[0]
+        pieces.append(layout.spread(after(slots[w], *packed)))
+
+    prompt_keys = 8 * prompt_rows
+    response_keys = layout.rings * 2 * rows
     chunk = divisor(prompt_keys, 512, 256, 128)
     finished = []
     for w in range(cands):
-        units = (w * 2, w * 2 + 1)
         state = kernel_call(
-            functools.partial(prompt_kernel, layout, units, chunk),
+            functools.partial(prompt_kernel, layout, (w * 2, w * 2 + 1), chunk),
             [
                 struct(2, HEAD, queries, dtype=jnp.float32),
                 struct(2, 1, queries, dtype=jnp.float32),
                 struct(2, 1, queries, dtype=jnp.float32),
             ],
-            (info, *asked, *prompt),
+            (info, *packed),
             scratch=[bf16((prompt_keys, HEAD))] * 2 + [bf16((queries, HEAD))],
             cost=(8 * queries * prompt_keys * HEAD, 4 * prompt_keys * HEAD),
             name="prompt_part",
             spare=12 << 20,
         )
-        response_keys = layout.rings * 2 * rows
-        outs = kernel_call(
-            functools.partial(response_kernel, layout, w, divisor(response_keys, 384, 256, 128)),
-            [struct(rows, WIDE)] * 4,
-            (info, *asked, *state, *pieces[w]),
-            scratch=[bf16((response_keys, HEAD))] * 2 + [bf16((queries, HEAD))],
-            cost=(8 * queries * response_keys * HEAD, 4 * response_keys * HEAD),
-            name="response_part",
-            spare=12 << 20,
-        )
+        outs = [None] * 4
+        for dx in (1, 0):
+            outs[dx * 2], outs[dx * 2 + 1] = kernel_call(
+                functools.partial(
+                    response_kernel, layout, w, dx, divisor(response_keys, 384, 256, 128)
+                ),
+                [struct(rows, WIDE)] * 2,
+                (info, *packed, *state, *pieces[w]),
+                scratch=[bf16((response_keys, HEAD))] * 2 + [bf16((queries, HEAD))],
+                cost=(4 * queries * response_keys * HEAD, 2 * response_keys * HEAD),
+                name="response_part",
+                spare=12 << 20,
+            )
         finished += layout.exchange(outs)
-    return kernel_call(
-        join_kernel, struct(*q.shape), finished, name="join_heads", scalars=0
-    )
+    return kernel_call(join_kernel, struct(*q.shape), finished, name="join_heads", scalars=0)
 
 
 def solution(mesh):

time: 100 us -> 94.5 us (0.945)
  the two profiles are of different devices: /device:TPU:12 before, /device:TPU:0 now
where the time goes in v3:
time: 94.5 us; the launch traced here: 93.1 us
  starting transfers between devices  34.8 us (37%)
  waiting for transfers between devices  27.6 us (29%)
  Pallas kernels  26.3 us (28%)
  local copies, waits for them, and re-layouts  4.19 us (4%)
    ppermute x29, starting transfers between devices, permute(): return lax.ppermute(array, AXES, pairs)  34.8 us
    ppermute x29, waiting for transfers between devices, permute(): return lax.ppermute(array, AXES, pairs)  27.6 us
    pallas_call x10, Pallas kernels, kernel_call(): pl.pallas_call(kernel, out_shape=out_shape, in_specs=[SMEM] * scalars + [...  25 us
    unnamed x9, local copies, waits for them, and re-layouts  3.35 us
  transfers between devices with their start and end apart: 29, of which 8 were waited for; matrix products, arithmetic and copies ran while one was open for 2% of the time, Pallas kernels for 27%

profile of v3, /device:TPU:0, one launch (start us, length us, event | category | flops | bytes accessed | tf_op | source)
XLA Modules:
  0.0 93.1 jit_solution(2794528515003868979)
XLA Ops:
  1.9 3.0 %collective-permute-start = (bf16[192,256]{1,0:T(8,128)(2,1)S(1)}, bf16[192,256]{1,0:T(8,128)(2,1)S(1)}, u32[]{:S(2)}, u32[]{:S(2)}) collective-permute-start(bf16[192,256]{1,0:T(8,128)(2,1)S(1)} %get-tuple-element.32), channel_id=1, source_target_pairs={{0,1},{1,0},{2,3},{3,2},{4,5},{5,4},{6,7},{7,6},{8,9},{9,8},{10,11... | collective-permute-start | bytes 294920 | tf_op jit(solution)/shard_map/ppermute | solution.py:40
  5.0 1.5 %collective-permute-start.1 = (bf16[192,256]{1,0:T(8,128)(2,1)S(1)}, bf16[192,256]{1,0:T(8,128)(2,1)S(1)}, u32[]{:S(2)}, u32[]{:S(2)}) collective-permute-start(bf16[192,256]{1,0:T(8,128)(2,1)S(1)} %get-tuple-element.33), channel_id=1, source_target_pairs={{0,16},{1,17},{2,18},{3,19},{4,20},{5,21},{6,22},{7,23},{8,24},{9,... | collective-permute-start | bytes 294920 | tf_op jit(solution)/shard_map/ppermute | solution.py:40
  8.7 2.0 %collective-permute-start.7 = (bf16[64,1024]{1,0:T(8,128)(2,1)S(1)}, bf16[64,1024]{1,0:T(8,128)(2,1)S(1)}, u32[]{:S(2)}, u32[]{:S(2)}) collective-permute-start(bf16[64,1024]{1,0:T(8,128)(2,1)S(1)} %constant_dynamic-update-slice_fusion.refs_0_), channel_id=1, source_target_pairs={{0,2},{1,3},{2,4},{3,5},{4,6},{5,7},{6,0},{7,1},{8,10},{9,11},{10,... | collective-permute-start | bytes 393224 | tf_op jit(solution)/shard_map/ppermute | solution.py:40
  10.7 2.6 %collective-permute-start.8 = (bf16[64,1024]{1,0:T(8,128)(2,1)S(1)}, bf16[64,1024]{1,0:T(8,128)(2,1)S(1)}, u32[]{:S(2)}, u32[]{:S(2)}) collective-permute-start(bf16[64,1024]{1,0:T(8,128)(2,1)S(1)} %constant_dynamic-update-slice_fusion.refs_0_), channel_id=1, source_target_pairs={{0,4},{1,5},{2,6},{3,7},{4,0},{5,1},{6,2},{7,3},{8,12},{9,13},{10,... | collective-permute-start | bytes 393224 | tf_op jit(solution)/shard_map/ppermute | solution.py:40
  13.3 2.3 %collective-permute-start.9 = (bf16[64,1024]{1,0:T(8,128)(2,1)S(1)}, bf16[64,1024]{1,0:T(8,128)(2,1)S(1)}, u32[]{:S(2)}, u32[]{:S(2)}) collective-permute-start(bf16[64,1024]{1,0:T(8,128)(2,1)S(1)} %constant_dynamic-update-slice_fusion.refs_0_), channel_id=1, source_target_pairs={{0,6},{1,7},{2,0},{3,1},{4,2},{5,3},{6,4},{7,5},{8,14},{9,15},{10,... | collective-permute-start | bytes 393224 | tf_op jit(solution)/shard_map/ppermute | solution.py:40
  18.7 3.6 %collective-permute-done.8.refs_2_ = bf16[64,1024]{1,0:T(8,128)(2,1)S(1)} collective-permute-done((bf16[64,1024]{1,0:T(8,128)(2,1)S(1)}, bf16[64,1024]{1,0:T(8,128)(2,1)S(1)}, u32[]{:S(2)}, u32[]{:S(2)}) %collective-permute-start.8) | collective-permute-done | bytes 131104 | tf_op jit(solution)/shard_map/ppermute | solution.py:40
  22.7 1.6 %collective-permute-start.10 = (bf16[1472,128]{1,0:T(8,128)(2,1)S(1)}, bf16[1472,128]{1,0:T(8,128)(2,1)S(1)}, u32[]{:S(2)}, u32[]{:S(2)}) collective-permute-start(bf16[1472,128]{1,0:T(8,128)(2,1)S(1)} %get-tuple-element.38), channel_id=1, source_target_pairs={{0,1},{1,0},{2,3},{3,2},{4,5},{5,4},{6,7},{7,6},{8,9},{9,8},{10,11... | collective-permute-start | bytes 1130504 | tf_op jit(solution)/shard_map/ppermute | solution.py:40
  26.2 3.3 %collective-permute-start.17 = (bf16[2,2,96,256]{3,2,1,0:T(8,128)(2,1)S(1)}, bf16[2,2,96,256]{3,2,1,0:T(8,128)(2,1)S(1)}, u32[]{:S(2)}, u32[]{:S(2)}) collective-permute-start(bf16[2,2,96,256]{3,2,1,0:T(8,128)(2,1)S(1)} %get-tuple-element.35.refs_11_), channel_id=1, source_target_pairs={{0,2},{1,3},{2,4},{3,5},{4,6},{5,7},{6,0},{7,1},{8,10},{9,11},{10,... | collective-permute-start | bytes 589832 | tf_op jit(solution)/shard_map/ppermute | solution.py:40
  29.5 4.0 %collective-permute-done.10.refs_1_ = bf16[1472,128]{1,0:T(8,128)(2,1)S(1)} collective-permute-done((bf16[1472,128]{1,0:T(8,128)(2,1)S(1)}, bf16[1472,128]{1,0:T(8,128)(2,1)S(1)}, u32[]{:S(2)}, u32[]{:S(2)}) %collective-permute-start.10) | collective-permute-done | bytes 376864 | tf_op jit(solution)/shard_map/ppermute | solution.py:40
  33.5 2.4 %collective-permute-done.11.refs_2_ = bf16[1472,128]{1,0:T(8,128)(2,1)S(1)} collective-permute-done((bf16[1472,128]{1,0:T(8,128)(2,1)S(1)}, bf16[1472,128]{1,0:T(8,128)(2,1)S(1)}, u32[]{:S(2)}, u32[]{:S(2)}) %collective-permute-start.11) | collective-permute-done | bytes 376864 | tf_op jit(solution)/shard_map/ppermute | solution.py:40
  36.0 6.7 %collective-permute-done.12.refs_3_ = bf16[1472,128]{1,0:T(8,128)(2,1)S(1)} collective-permute-done((bf16[1472,128]{1,0:T(8,128)(2,1)S(1)}, bf16[1472,128]{1,0:T(8,128)(2,1)S(1)}, u32[]{:S(2)}, u32[]{:S(2)}) %collective-permute-start.12) | collective-permute-done | bytes 376864 | tf_op jit(solution)/shard_map/ppermute | solution.py:40
  42.6 3.4 %collective-permute-start.18 = (bf16[2,2,96,256]{3,2,1,0:T(8,128)(2,1)S(1)}, bf16[2,2,96,256]{3,2,1,0:T(8,128)(2,1)S(1)}, u32[]{:S(2)}, u32[]{:S(2)}) collective-permute-start(bf16[2,2,96,256]{3,2,1,0:T(8,128)(2,1)S(1)} %collective-permute-done.17.refs_12_), channel_id=1, source_target_pairs={{0,2},{1,3},{2,4},{3,5},{4,6},{5,7},{6,0},{7,1},{8,10},{9,11},{10,... | collective-permute-start | bytes 589832 | tf_op jit(solution)/shard_map/ppermute | solution.py:40
  46.0 6.1 %collective-permute-done.18.refs_13_ = bf16[2,2,96,256]{3,2,1,0:T(8,128)(2,1)S(1)} collective-permute-done((bf16[2,2,96,256]{3,2,1,0:T(8,128)(2,1)S(1)}, bf16[2,2,96,256]{3,2,1,0:T(8,128)(2,1)S(1)}, u32[]{:S(2)}, u32[]{:S(2)}) %collective-permute-start.18) | collective-permute-done | bytes 196640 | tf_op jit(solution)/shard_map/ppermute | solution.py:40
  53.7 2.9 %collective-permute-start.24 = (bf16[2,2,96,256]{3,2,1,0:T(8,128)(2,1)S(1)}, bf16[2,2,96,256]{3,2,1,0:T(8,128)(2,1)S(1)}, u32[]{:S(2)}, u32[]{:S(2)}) collective-permute-start(bf16[2,2,96,256]{3,2,1,0:T(8,128)(2,1)S(1)} %get-tuple-element.52.refs_11_), channel_id=1, source_target_pairs={{0,4},{1,5},{2,6},{3,7},{4,0},{5,1},{6,2},{7,3},{8,12},{9,13},{10,... | collective-permute-start | bytes 589832 | tf_op jit(solution)/shard_map/ppermute | solution.py:40
  57.4 5.7 %prompt_part.2 = (f32[2,128,960]{2,1,0:T(8,128)S(1)}, f32[2,1,960]{2,1,0:T(1,128)S(1)}, f32[2,1,960]{2,1,0:T(1,128)S(1)}) custom-call(s32[24]{0:T(128)S(1)} %copy-done.3, bf16[1472,128]{1,0:T(8,128)(2,1)S(1)} %get-tuple-element.37.refs_0_, bf16[1472,128]{1,0:T(8,128)(2,1)S(1)} %collective-permute-done.10.refs_1_, ...), custom_call_target="tpu_custom_call" | custom-call | flops 2013265920 | bytes 1048576 | tf_op jit(solution)/shard_map/prompt_part/pallas_call | solution.py:59
  63.1 2.1 %response_part.5 = (bf16[96,640]{1,0:T(8,128)(2,1)S(1)}, bf16[96,640]{1,0:T(8,128)(2,1)S(1)}) custom-call(s32[24]{0:T(128)S(1)} %copy-done.3, bf16[1472,128]{1,0:T(8,128)(2,1)S(1)} %get-tuple-element.37.refs_0_, bf16[1472,128]{1,0:T(8,128)(2,1)S(1)} %collective-permute-done.10.refs_1_, bf16[1472,128]{1,0:T(8,128)(2,1)S(1)} %collective-permute-done.11.refs_2_, ...), custom_call_target="tpu_custom_call" | custom-call | flops 377487360 | bytes 196608 | tf_op jit(solution)/shard_map/response_part/pallas_call | solution.py:59
  65.2 1.6 %collective-permute-start.21 = (bf16[96,640]{1,0:T(8,128)(2,1)S(1)}, bf16[96,640]{1,0:T(8,128)(2,1)S(1)}, u32[]{:S(2)}, u32[]{:S(2)}) collective-permute-start(bf16[96,640]{1,0:T(8,128)(2,1)S(1)} %get-tuple-element.46), channel_id=1, source_target_pairs={{0,16},{1,17},{2,18},{3,19},{4,20},{5,21},{6,22},{7,23},{8,24},{9,... | collective-permute-start | bytes 368648 | tf_op jit(solution)/shard_map/ppermute | solution.py:40
  68.2 9.0 %prompt_part.3 = (f32[2,128,960]{2,1,0:T(8,128)S(1)}, f32[2,1,960]{2,1,0:T(1,128)S(1)}, f32[2,1,960]{2,1,0:T(1,128)S(1)}) custom-call(s32[24]{0:T(128)S(1)} %copy-done.3, bf16[1472,128]{1,0:T(8,128)(2,1)S(1)} %get-tuple-element.37.refs_0_, bf16[1472,128]{1,0:T(8,128)(2,1)S(1)} %collective-permute-done.10.refs_1_, ...), custom_call_target="tpu_custom_call" | custom-call | flops 2013265920 | bytes 1048576 | tf_op jit(solution)/shard_map/prompt_part/pallas_call | solution.py:59
  77.2 2.1 %response_part.4 = (bf16[96,640]{1,0:T(8,128)(2,1)S(1)}, bf16[96,640]{1,0:T(8,128)(2,1)S(1)}) custom-call(s32[24]{0:T(128)S(1)} %copy-done.3, bf16[1472,128]{1,0:T(8,128)(2,1)S(1)} %get-tuple-element.37.refs_0_, bf16[1472,128]{1,0:T(8,128)(2,1)S(1)} %collective-permute-done.10.refs_1_, bf16[1472,128]{1,0:T(8,128)(2,1)S(1)} %collective-permute-done.11.refs_2_, ...), custom_call_target="tpu_custom_call" | custom-call | flops 377487360 | bytes 196608 | tf_op jit(solution)/shard_map/response_part/pallas_call | solution.py:59
  79.9 2.1 %response_part.7 = (bf16[96,640]{1,0:T(8,128)(2,1)S(1)}, bf16[96,640]{1,0:T(8,128)(2,1)S(1)}) custom-call(s32[24]{0:T(128)S(1)} %copy-done.3, bf16[1472,128]{1,0:T(8,128)(2,1)S(1)} %get-tuple-element.37.refs_0_, bf16[1472,128]{1,0:T(8,128)(2,1)S(1)} %collective-permute-done.10.refs_1_, bf16[1472,128]{1,0:T(8,128)(2,1)S(1)} %collective-permute-done.11.refs_2_, ...), custom_call_target="tpu_custom_call" | custom-call | flops 377487360 | bytes 196608 | tf_op jit(solution)/shard_map/response_part/pallas_call | solution.py:59
  82.0 1.6 %collective-permute-start.27 = (bf16[96,640]{1,0:T(8,128)(2,1)S(1)}, bf16[96,640]{1,0:T(8,128)(2,1)S(1)}, u32[]{:S(2)}, u32[]{:S(2)}) collective-permute-start(bf16[96,640]{1,0:T(8,128)(2,1)S(1)} %get-tuple-element.55), channel_id=1, source_target_pairs={{0,16},{1,17},{2,18},{3,19},{4,20},{5,21},{6,22},{7,23},{8,24},{9,... | collective-permute-start | bytes 368648 | tf_op jit(solution)/shard_map/ppermute | solution.py:40
  85.0 2.1 %response_part.6 = (bf16[96,640]{1,0:T(8,128)(2,1)S(1)}, bf16[96,640]{1,0:T(8,128)(2,1)S(1)}) custom-call(s32[24]{0:T(128)S(1)} %copy-done.3, bf16[1472,128]{1,0:T(8,128)(2,1)S(1)} %get-tuple-element.37.refs_0_, bf16[1472,128]{1,0:T(8,128)(2,1)S(1)} %collective-permute-done.10.refs_1_, bf16[1472,128]{1,0:T(8,128)(2,1)S(1)} %collective-permute-done.11.refs_2_, ...), custom_call_target="tpu_custom_call" | custom-call | flops 377487360 | bytes 196608 | tf_op jit(solution)/shard_map/response_part/pallas_call | solution.py:59
  87.7 1.7 %collective-permute-done.28.refs_7_ = bf16[96,640]{1,0:T(8,128)(2,1)S(1)} collective-permute-done((bf16[96,640]{1,0:T(8,128)(2,1)S(1)}, bf16[96,640]{1,0:T(8,128)(2,1)S(1)}, u32[]{:S(2)}, u32[]{:S(2)}) %collective-permute-start.28) | collective-permute-done | bytes 122912 | tf_op jit(solution)/shard_map/ppermute | solution.py:40
  89.4 2.6 %collective-permute-done.26.refs_5_ = bf16[96,640]{1,0:T(8,128)(2,1)S(1)} collective-permute-done((bf16[96,640]{1,0:T(8,128)(2,1)S(1)}, bf16[96,640]{1,0:T(8,128)(2,1)S(1)}, u32[]{:S(2)}, u32[]{:S(2)}) %collective-permute-start.26) | collective-permute-done | bytes 122912 | tf_op jit(solution)/shard_map/ppermute | solution.py:40
  (55 shorter events, 17.2 us)
Async XLA Ops:
  1.9 5.8 %collective-permute-start = (bf16[192,256]{1,0:T(8,128)(2,1)S(1)}, bf16[192,256]{1,0:T(8,128)(2,1)S(1)}, u32[]{:S(2)}, u32[]{:S(2)}) collective-permute-start(bf16[192,256]{1,0:T(8,128)(2,1)S(1)} %get-tuple-element.32), channel_id=1, source_target_pairs={{0,1},{1,0},{2,3},{3,2},{4,5},{5,4},{6,7},{7,6},{8,9},{9,8},{10,11... | collective-permute-start | bytes 294920 | tf_op jit(solution)/shard_map/ppermute | solution.py:40
  6.5 6.9 %collective-permute-start.2 = (bf16[192,256]{1,0:T(8,128)(2,1)S(1)}, bf16[192,256]{1,0:T(8,128)(2,1)S(1)}, u32[]{:S(2)}, u32[]{:S(2)}) collective-permute-start(bf16[192,256]{1,0:T(8,128)(2,1)S(1)} %get-tuple-element.34), channel_id=1, source_target_pairs={{0,17},{1,16},{2,19},{3,18},{4,21},{5,20},{6,23},{7,22},{8,25},{9,... | collective-permute-start | bytes 294920 | tf_op jit(solution)/shard_map/ppermute | solution.py:40
  6.5 9.1 %collective-permute-start.3 = (bf16[192,256]{1,0:T(8,128)(2,1)S(1)}, bf16[192,256]{1,0:T(8,128)(2,1)S(1)}, u32[]{:S(2)}, u32[]{:S(2)}) collective-permute-start(bf16[192,256]{1,0:T(8,128)(2,1)S(1)} %get-tuple-element.31.refs_0_), channel_id=1, source_target_pairs={{0,8},{1,9},{2,10},{3,11},{4,12},{5,13},{6,14},{7,15},{8,0},{9,1},... | collective-permute-start | bytes 294920 | tf_op jit(solution)/shard_map/ppermute | solution.py:40
  7.8 7.8 %collective-permute-start.4 = (bf16[192,256]{1,0:T(8,128)(2,1)S(1)}, bf16[192,256]{1,0:T(8,128)(2,1)S(1)}, u32[]{:S(2)}, u32[]{:S(2)}) collective-permute-start(bf16[192,256]{1,0:T(8,128)(2,1)S(1)} %collective-permute-done.refs_1_), channel_id=1, source_target_pairs={{0,8},{1,9},{2,10},{3,11},{4,12},{5,13},{6,14},{7,15},{8,0},{9,1},... | collective-permute-start | bytes 294920 | tf_op jit(solution)/shard_map/ppermute | solution.py:40
  8.7 10.0 %collective-permute-start.7 = (bf16[64,1024]{1,0:T(8,128)(2,1)S(1)}, bf16[64,1024]{1,0:T(8,128)(2,1)S(1)}, u32[]{:S(2)}, u32[]{:S(2)}) collective-permute-start(bf16[64,1024]{1,0:T(8,128)(2,1)S(1)} %constant_dynamic-update-slice_fusion.refs_0_), channel_id=1, source_target_pairs={{0,2},{1,3},{2,4},{3,5},{4,6},{5,7},{6,0},{7,1},{8,10},{9,11},{10,... | collective-permute-start | bytes 393224 | tf_op jit(solution)/shard_map/ppermute | solution.py:40
  10.7 11.7 %collective-permute-start.8 = (bf16[64,1024]{1,0:T(8,128)(2,1)S(1)}, bf16[64,1024]{1,0:T(8,128)(2,1)S(1)}, u32[]{:S(2)}, u32[]{:S(2)}) collective-permute-start(bf16[64,1024]{1,0:T(8,128)(2,1)S(1)} %constant_dynamic-update-slice_fusion.refs_0_), channel_id=1, source_target_pairs={{0,4},{1,5},{2,6},{3,7},{4,0},{5,1},{6,2},{7,3},{8,12},{9,13},{10,... | collective-permute-start | bytes 393224 | tf_op jit(solution)/shard_map/ppermute | solution.py:40
  13.3 9.1 %collective-permute-start.9 = (bf16[64,1024]{1,0:T(8,128)(2,1)S(1)}, bf16[64,1024]{1,0:T(8,128)(2,1)S(1)}, u32[]{:S(2)}, u32[]{:S(2)}) collective-permute-start(bf16[64,1024]{1,0:T(8,128)(2,1)S(1)} %constant_dynamic-update-slice_fusion.refs_0_), channel_id=1, source_target_pairs={{0,6},{1,7},{2,0},{3,1},{4,2},{5,3},{6,4},{7,5},{8,14},{9,15},{10,... | collective-permute-start | bytes 393224 | tf_op jit(solution)/shard_map/ppermute | solution.py:40
  22.7 10.8 %collective-permute-start.10 = (bf16[1472,128]{1,0:T(8,128)(2,1)S(1)}, bf16[1472,128]{1,0:T(8,128)(2,1)S(1)}, u32[]{:S(2)}, u32[]{:S(2)}) collective-permute-start(bf16[1472,128]{1,0:T(8,128)(2,1)S(1)} %get-tuple-element.38), channel_id=1, source_target_pairs={{0,1},{1,0},{2,3},{3,2},{4,5},{5,4},{6,7},{7,6},{8,9},{9,8},{10,11... | collective-permute-start | bytes 1130504 | tf_op jit(solution)/shard_map/ppermute | solution.py:40
  24.3 11.7 %collective-permute-start.11 = (bf16[1472,128]{1,0:T(8,128)(2,1)S(1)}, bf16[1472,128]{1,0:T(8,128)(2,1)S(1)}, u32[]{:S(2)}, u32[]{:S(2)}) collective-permute-start(bf16[1472,128]{1,0:T(8,128)(2,1)S(1)} %get-tuple-element.39), channel_id=1, source_target_pairs={{0,16},{1,17},{2,18},{3,19},{4,20},{5,21},{6,22},{7,23},{8,24},{9,... | collective-permute-start | bytes 1130504 | tf_op jit(solution)/shard_map/ppermute | solution.py:40
  25.8 16.8 %collective-permute-start.12 = (bf16[1472,128]{1,0:T(8,128)(2,1)S(1)}, bf16[1472,128]{1,0:T(8,128)(2,1)S(1)}, u32[]{:S(2)}, u32[]{:S(2)}) collective-permute-start(bf16[1472,128]{1,0:T(8,128)(2,1)S(1)} %get-tuple-element.40), channel_id=1, source_target_pairs={{0,17},{1,16},{2,19},{3,18},{4,21},{5,20},{6,23},{7,22},{8,25},{9,... | collective-permute-start | bytes 1130504 | tf_op jit(solution)/shard_map/ppermute | solution.py:40
  26.2 16.4 %collective-permute-start.17 = (bf16[2,2,96,256]{3,2,1,0:T(8,128)(2,1)S(1)}, bf16[2,2,96,256]{3,2,1,0:T(8,128)(2,1)S(1)}, u32[]{:S(2)}, u32[]{:S(2)}) collective-permute-start(bf16[2,2,96,256]{3,2,1,0:T(8,128)(2,1)S(1)} %get-tuple-element.35.refs_11_), channel_id=1, source_target_pairs={{0,2},{1,3},{2,4},{3,5},{4,6},{5,7},{6,0},{7,1},{8,10},{9,11},{10,... | collective-permute-start | bytes 589832 | tf_op jit(solution)/shard_map/ppermute | solution.py:40
  29.5 23.8 %collective-permute-start.13 = (bf16[1472,128]{1,0:T(8,128)(2,1)S(1)}, bf16[1472,128]{1,0:T(8,128)(2,1)S(1)}, u32[]{:S(2)}, u32[]{:S(2)}) collective-permute-start(bf16[1472,128]{1,0:T(8,128)(2,1)S(1)} %get-tuple-element.37.refs_0_), channel_id=1, source_target_pairs={{0,8},{1,9},{2,10},{3,11},{4,12},{5,13},{6,14},{7,15},{8,0},{9,1},... | collective-permute-start | bytes 1130504 | tf_op jit(solution)/shard_map/ppermute | solution.py:40
  33.5 19.8 %collective-permute-start.14 = (bf16[1472,128]{1,0:T(8,128)(2,1)S(1)}, bf16[1472,128]{1,0:T(8,128)(2,1)S(1)}, u32[]{:S(2)}, u32[]{:S(2)}) collective-permute-start(bf16[1472,128]{1,0:T(8,128)(2,1)S(1)} %collective-permute-done.10.refs_1_), channel_id=1, source_target_pairs={{0,8},{1,9},{2,10},{3,11},{4,12},{5,13},{6,14},{7,15},{8,0},{9,1},... | collective-permute-start | bytes 1130504 | tf_op jit(solution)/shard_map/ppermute | solution.py:40
  35.9 17.4 %collective-permute-start.15 = (bf16[1472,128]{1,0:T(8,128)(2,1)S(1)}, bf16[1472,128]{1,0:T(8,128)(2,1)S(1)}, u32[]{:S(2)}, u32[]{:S(2)}) collective-permute-start(bf16[1472,128]{1,0:T(8,128)(2,1)S(1)} %collective-permute-done.11.refs_2_), channel_id=1, source_target_pairs={{0,8},{1,9},{2,10},{3,11},{4,12},{5,13},{6,14},{7,15},{8,0},{9,1},... | collective-permute-start | bytes 1130504 | tf_op jit(solution)/shard_map/ppermute | solution.py:40
  42.6 10.7 %collective-permute-start.16 = (bf16[1472,128]{1,0:T(8,128)(2,1)S(1)}, bf16[1472,128]{1,0:T(8,128)(2,1)S(1)}, u32[]{:S(2)}, u32[]{:S(2)}) collective-permute-start(bf16[1472,128]{1,0:T(8,128)(2,1)S(1)} %collective-permute-done.12.refs_3_), channel_id=1, source_target_pairs={{0,8},{1,9},{2,10},{3,11},{4,12},{5,13},{6,14},{7,15},{8,0},{9,1},... | collective-permute-start | bytes 1130504 | tf_op jit(solution)/shard_map/ppermute | solution.py:40
  42.6 9.5 %collective-permute-start.18 = (bf16[2,2,96,256]{3,2,1,0:T(8,128)(2,1)S(1)}, bf16[2,2,96,256]{3,2,1,0:T(8,128)(2,1)S(1)}, u32[]{:S(2)}, u32[]{:S(2)}) collective-permute-start(bf16[2,2,96,256]{3,2,1,0:T(8,128)(2,1)S(1)} %collective-permute-done.17.refs_12_), channel_id=1, source_target_pairs={{0,2},{1,3},{2,4},{3,5},{4,6},{5,7},{6,0},{7,1},{8,10},{9,11},{10,... | collective-permute-start | bytes 589832 | tf_op jit(solution)/shard_map/ppermute | solution.py:40
  52.1 11.0 %collective-permute-start.19 = (bf16[2,2,96,256]{3,2,1,0:T(8,128)(2,1)S(1)}, bf16[2,2,96,256]{3,2,1,0:T(8,128)(2,1)S(1)}, u32[]{:S(2)}, u32[]{:S(2)}) collective-permute-start(bf16[2,2,96,256]{3,2,1,0:T(8,128)(2,1)S(1)} %collective-permute-done.18.refs_13_), channel_id=1, source_target_pairs={{0,2},{1,3},{2,4},{3,5},{4,6},{5,7},{6,0},{7,1},{8,10},{9,11},{10,... | collective-permute-start | bytes 589832 | tf_op jit(solution)/shard_map/ppermute | solution.py:40
  53.3 26.0 %collective-permute-start.23 = (bf16[2,2,96,256]{3,2,1,0:T(8,128)(2,1)S(1)}, bf16[2,2,96,256]{3,2,1,0:T(8,128)(2,1)S(1)}, u32[]{:S(2)}, u32[]{:S(2)}) collective-permute-start(bf16[2,2,96,256]{3,2,1,0:T(8,128)(2,1)S(1)} %get-tuple-element.52.refs_11_), channel_id=1, source_target_pairs={{0,2},{1,3},{2,4},{3,5},{4,6},{5,7},{6,0},{7,1},{8,10},{9,11},{10,... | collective-permute-start | bytes 589832 | tf_op jit(solution)/shard_map/ppermute | solution.py:40
  53.7 26.3 %collective-permute-start.24 = (bf16[2,2,96,256]{3,2,1,0:T(8,128)(2,1)S(1)}, bf16[2,2,96,256]{3,2,1,0:T(8,128)(2,1)S(1)}, u32[]{:S(2)}, u32[]{:S(2)}) collective-permute-start(bf16[2,2,96,256]{3,2,1,0:T(8,128)(2,1)S(1)} %get-tuple-element.52.refs_11_), channel_id=1, source_target_pairs={{0,4},{1,5},{2,6},{3,7},{4,0},{5,1},{6,2},{7,3},{8,12},{9,13},{10,... | collective-permute-start | bytes 589832 | tf_op jit(solution)/shard_map/ppermute | solution.py:40
  56.5 23.4 %collective-permute-start.25 = (bf16[2,2,96,256]{3,2,1,0:T(8,128)(2,1)S(1)}, bf16[2,2,96,256]{3,2,1,0:T(8,128)(2,1)S(1)}, u32[]{:S(2)}, u32[]{:S(2)}) collective-permute-start(bf16[2,2,96,256]{3,2,1,0:T(8,128)(2,1)S(1)} %get-tuple-element.52.refs_11_), channel_id=1, source_target_pairs={{0,6},{1,7},{2,0},{3,1},{4,2},{5,3},{6,4},{7,5},{8,14},{9,15},{10,... | collective-permute-start | bytes 589832 | tf_op jit(solution)/shard_map/ppermute | solution.py:40
  65.2 21.9 %collective-permute-start.21 = (bf16[96,640]{1,0:T(8,128)(2,1)S(1)}, bf16[96,640]{1,0:T(8,128)(2,1)S(1)}, u32[]{:S(2)}, u32[]{:S(2)}) collective-permute-start(bf16[96,640]{1,0:T(8,128)(2,1)S(1)} %get-tuple-element.46), channel_id=1, source_target_pairs={{0,16},{1,17},{2,18},{3,19},{4,20},{5,21},{6,22},{7,23},{8,24},{9,... | collective-permute-start | bytes 368648 | tf_op jit(solution)/shard_map/ppermute | solution.py:40
  66.7 20.9 %collective-permute-start.22 = (bf16[96,640]{1,0:T(8,128)(2,1)S(1)}, bf16[96,640]{1,0:T(8,128)(2,1)S(1)}, u32[]{:S(2)}, u32[]{:S(2)}) collective-permute-start(bf16[96,640]{1,0:T(8,128)(2,1)S(1)} %get-tuple-element.47), channel_id=1, source_target_pairs={{0,17},{1,16},{2,19},{3,18},{4,21},{5,20},{6,23},{7,22},{8,25},{9,... | collective-permute-start | bytes 368648 | tf_op jit(solution)/shard_map/ppermute | solution.py:40
  79.3 8.4 %collective-permute-start.20 = (bf16[96,640]{1,0:T(8,128)(2,1)S(1)}, bf16[96,640]{1,0:T(8,128)(2,1)S(1)}, u32[]{:S(2)}, u32[]{:S(2)}) collective-permute-start(bf16[96,640]{1,0:T(8,128)(2,1)S(1)} %get-tuple-element.45), channel_id=1, source_target_pairs={{0,1},{1,0},{2,3},{3,2},{4,5},{5,4},{6,7},{7,6},{8,9},{9,8},{10,11... | collective-permute-start | bytes 368648 | tf_op jit(solution)/shard_map/ppermute | solution.py:40
  83.5 5.9 %collective-permute-start.28 = (bf16[96,640]{1,0:T(8,128)(2,1)S(1)}, bf16[96,640]{1,0:T(8,128)(2,1)S(1)}, u32[]{:S(2)}, u32[]{:S(2)}) collective-permute-start(bf16[96,640]{1,0:T(8,128)(2,1)S(1)} %get-tuple-element.56), channel_id=1, source_target_pairs={{0,17},{1,16},{2,19},{3,18},{4,21},{5,20},{6,23},{7,22},{8,25},{9,... | collective-permute-start | bytes 368648 | tf_op jit(solution)/shard_map/ppermute | solution.py:40
  (9 other events, 43.1 us)
